TPU v7x, 256 devices: a whole 4x4x8 slice. The times are simulated.
256 devices in a mesh: ctx: 32 (over y, z), tp: 8 (over x, core).
Axes of the slice: x: 4, y: 4, z: 8, core: 2. Of those that a mesh axis runs over, the one named last changes fastest.
Arguments:
- ssm_inputs: bfloat16 [8192, 8192], P('ctx', 'tp'), may hold values from -4 to 4
- state_maps: bfloat16 [8192, 8, 256], P('ctx', 'tp'), may hold values from -4 to 4
- ssm_gates: bfloat16 [8192, 8192], P('ctx', 'tp'), may hold values from -4 to 4
- time_steps: float32 [128, 8192], P('tp', 'ctx'), may hold values from -5 to 512
- log_rates: float32 [128], P('tp'), may hold values from -12 to 1
- skip_gain: float32 [128], P('tp'), may hold values from 0.5 to 2
- conv_inputs: bfloat16 [4, 8192], P(None, 'tp'), may hold values from -3 to 3
- conv_maps: bfloat16 [4, 8, 256], P(None, 'tp'), may hold values from -3 to 3
- norm_gain: float32 [8192], P('tp'), may hold values from 0.1 to 1.9
- out_weight: bfloat16 [8192, 4096], P('tp'), may hold values from -0.0625 to 0.0625
- queries: bfloat16 [8192, 8192], P('ctx', 'tp'), may hold values from -5 to 5
- attention_keys: bfloat16 [8192, 1024], P('ctx', 'tp'), may hold values from -5 to 5
- values: bfloat16 [8192, 1024], P('ctx', 'tp'), may hold values from -4 to 4
Outputs:
- ssm_out: bfloat16 [8192, 4096], P(('ctx', 'tp'))
- attn_out: bfloat16 [8192, 8192], P('ctx', 'tp')
All inputs are finite; a program needn't handle non-finite values.
Results may differ from a plain program's by a relative error of at most 0.03.
Values may be sent and summed in bfloat16 or wider, within the bound.
No kernel may reach another device: no remote copies, remote signals or barrier semaphores. Data moves between devices by JAX's collectives and lax.ppermute only.
A program may use at most 128 MiB of HBM per device.

v0:
```python
import jax
import jax.numpy as jnp
from jax import lax
from jax.sharding import PartitionSpec as P

QUERY_HEADS = 64
KEY_VALUE_HEADS = 8
HEAD_SIZE = 128


def passed_along(shard, axis, by):
    size = lax.axis_size(axis)
    pairs = [(i, i + by) for i in range(size) if 0 <= i + by < size]
    return lax.ppermute(shard, axis, pairs)


def prefix_2(shard, axis, join, neutral):
    place = lax.axis_index(axis)
    gathered = jax.tree.map(
        lambda a, kind: lax.all_gather(a.astype(kind), axis), shard, (jnp.bfloat16, jnp.bfloat16)
    )
    state = jax.tree.map(lambda a, e: jnp.zeros_like(a) + jnp.asarray(e, a.dtype), shard, neutral)

    def one(step, state):
        return join(
            state,
            jax.tree.map(
                lambda a, own: lax.dynamic_index_in_dim(a, step, 0, False).astype(own.dtype),
                gathered,
                shard,
            ),
        )

    return lax.fori_loop(0, place, one, state)


def conv_silu(extended, conv_taps, tok_rows):
    summed = jnp.zeros((tok_rows,) + extended.shape[1:], jnp.float32)
    for tap_index in range(conv_taps.shape[0]):
        summed = summed + conv_taps[tap_index].astype(jnp.float32) * extended[
            tap_index : tap_index + tok_rows
        ].astype(jnp.float32)
    return jax.nn.silu(summed).astype(jnp.bfloat16)


def per_device(
    ssm_inputs,
    state_maps,
    ssm_gates,
    time_steps,
    log_rates,
    skip_gain,
    conv_inputs,
    conv_maps,
    norm_gain,
    out_weight,
    queries,
    attention_keys,
    values,
):
    tok_rows = ssm_inputs.shape[0]
    tap_count = conv_inputs.shape[0]
    groups_here = state_maps.shape[1]
    state_size = state_maps.shape[2] // 2
    heads_here = log_rates.shape[0]
    per_group = heads_here // groups_here
    head_dim = ssm_inputs.shape[1] // heads_here
    my_index = lax.axis_index("ctx")
    lead_inputs, lead_maps = passed_along(
        (ssm_inputs[tok_rows - tap_count + 1 :], state_maps[tok_rows - tap_count + 1 :]), "ctx", 1
    )
    mixed_inputs = conv_silu(
        jnp.concatenate([lead_inputs, ssm_inputs], axis=0), conv_inputs, tok_rows
    )
    mixed_maps = conv_silu(jnp.concatenate([lead_maps, state_maps], axis=0), conv_maps, tok_rows)
    input_heads = mixed_inputs.reshape(tok_rows, groups_here, per_group, head_dim)
    b_maps = mixed_maps[:, :, :state_size]
    c_maps = mixed_maps[:, :, state_size:]
    step_sizes = jax.nn.softplus(time_steps).reshape(groups_here, per_group, tok_rows)
    decline_rate = -jnp.exp(log_rates).reshape(groups_here, per_group)
    running_log = jnp.cumsum(step_sizes * decline_rate[:, :, None], axis=2)
    map_products = jnp.einsum("tgn,sgn->gts", c_maps, b_maps, preferred_element_type=jnp.float32)
    token_location = jnp.arange(tok_rows)
    causal = token_location[:, None] >= token_location[None, :]
    log_gap = running_log[:, :, :, None] - running_log[:, :, None, :]
    decay_table = jnp.where(causal, jnp.exp(jnp.minimum(log_gap, 0.0)), 0.0)
    mixer = (map_products[:, None] * decay_table * step_sizes[:, :, None, :]).astype(jnp.bfloat16)
    inner_part = jnp.einsum(
        "gjts,sgjp->tgjp", mixer, input_heads, preferred_element_type=jnp.float32
    )
    inputs_float = input_heads.astype(jnp.float32)
    tail_weight = jnp.exp(running_log[:, :, -1:] - running_log) * step_sizes
    weighted = (jnp.transpose(tail_weight, (2, 0, 1))[..., None] * inputs_float).astype(
        jnp.bfloat16
    )
    block_state = jnp.einsum("sgjp,sgn->gjpn", weighted, b_maps, preferred_element_type=jnp.float32)
    block_decay = running_log[:, :, -1]

    def combine(earlier, later):
        return (earlier[0] + later[0], jnp.exp(later[0])[:, :, None, None] * earlier[1] + later[1])

    prefix = prefix_2(
        (block_decay, block_state),
        "ctx",
        combine,
        (jnp.zeros_like(block_decay), jnp.zeros_like(block_state)),
    )
    entering = prefix[1]
    carried = jnp.einsum(
        "tgn,gjpn->tgjp", c_maps.astype(jnp.float32), entering, precision=lax.Precision.HIGHEST
    )
    outside = jnp.transpose(jnp.exp(running_log), (2, 0, 1))[..., None] * carried
    ssm_output = (
        inner_part
        + outside
        + skip_gain.reshape(groups_here, per_group)[None, :, :, None] * inputs_float
    )
    channel_count = per_group * head_dim
    gated = ssm_output.reshape(tok_rows, groups_here, channel_count) * jax.nn.silu(
        ssm_gates.reshape(tok_rows, groups_here, channel_count).astype(jnp.float32)
    )
    mean_square = jnp.mean(gated * gated, axis=2, keepdims=True)
    normed = (
        (gated * lax.rsqrt(mean_square + 1e-05)).reshape(tok_rows, groups_here * channel_count)
        * norm_gain
    ).astype(jnp.bfloat16)
    ssm_out = lax.psum_scatter(
        jnp.dot(normed, out_weight, preferred_element_type=jnp.float32).astype(jnp.bfloat16),
        "tp",
        scatter_dimension=0,
        tiled=True,
    )
    kv_heads = attention_keys.shape[1] // HEAD_SIZE
    shared_heads = QUERY_HEADS // KEY_VALUE_HEADS
    score_scale = HEAD_SIZE ** (-0.5)
    query_pos = my_index * tok_rows + token_location
    query_heads = queries.reshape(tok_rows, kv_heads, shared_heads, HEAD_SIZE)
    block_rows = tok_rows // 4
    first_key = jnp.int32(0)
    key_block = lax.all_gather(attention_keys, "ctx", axis=0, tiled=True)
    value_block = lax.all_gather(values, "ctx", axis=0, tiled=True)
    key_count = key_block.shape[0]
    key_head_rows = key_block.reshape(key_count, kv_heads, HEAD_SIZE)
    value_head_rows = value_block.reshape(key_count, kv_heads, HEAD_SIZE)
    key_pos = jnp.arange(key_count)
    peaks = jnp.full((kv_heads, shared_heads, tok_rows), -1e30, jnp.float32)
    totals = jnp.zeros((kv_heads, shared_heads, tok_rows), jnp.float32)
    sums = jnp.zeros((kv_heads, shared_heads, tok_rows, HEAD_SIZE), jnp.float32)
    new_parts = []
    for current_block_index in range(4):
        row_lower = current_block_index * block_rows
        row_upper = row_lower + block_rows
        query_tile_block = query_heads[row_lower:row_upper]
        block_pos = query_pos[row_lower:row_upper]
        old_state = (
            peaks[:, :, row_lower:row_upper],
            totals[:, :, row_lower:row_upper],
            sums[:, :, row_lower:row_upper],
        )

        def update(old_part, query_tile_block=query_tile_block, block_pos=block_pos):
            old_peak, old_total, old_sum = old_part
            scores = (
                jnp.einsum(
                    "bgrd,kgd->grbk",
                    query_tile_block,
                    key_head_rows,
                    preferred_element_type=jnp.float32,
                )
                * score_scale
            )
            allowed = key_pos[None, :] <= block_pos[:, None]
            scores = jnp.where(allowed, scores, -1e30)
            new_peak = jnp.maximum(old_peak, jnp.max(scores, axis=3))
            weights = jnp.where(allowed, jnp.exp(scores - new_peak[..., None]), 0.0)
            new_total = jnp.sum(weights, axis=3)
            new_sum = jnp.einsum(
                "grbk,kgd->grbd",
                weights.astype(jnp.bfloat16),
                value_head_rows,
                preferred_element_type=jnp.float32,
            )
            return (new_peak, new_total, new_sum)

        def unchanged(old_part):
            return old_part

        new_parts.append(
            lax.cond(block_pos[block_rows - 1] >= first_key, update, unchanged, old_state)
        )
    peaks, totals, sums = tuple(
        (
            jnp.concatenate([block_part[member] for block_part in new_parts], axis=2)
            for member in range(3)
        )
    )
    attended = sums / totals[..., None]
    attn_out = (
        jnp.transpose(attended, (2, 0, 1, 3))
        .reshape(tok_rows, kv_heads * shared_heads * HEAD_SIZE)
        .astype(jnp.bfloat16)
    )
    return (ssm_out, attn_out)


def solution(mesh):
    placed = (
        P("ctx", "tp"),
        P("ctx", "tp", None),
        P("ctx", "tp"),
        P("tp", "ctx"),
        P("tp"),
        P("tp"),
        P(None, "tp"),
        P(None, "tp", None),
        P("tp"),
        P("tp", None),
        P("ctx", "tp"),
        P("ctx", "tp"),
        P("ctx", "tp"),
    )
    return jax.shard_map(
        per_device,
        mesh=mesh,
        in_specs=placed,
        out_specs=(P(("ctx", "tp"), None), P("ctx", "tp")),
        check_vma=False,
    )
```

profile of v0, /device:TPU:4, one launch (start us, length us, event | category | flops | bytes accessed | tf_op | source)
XLA Modules:
  0.0 351.8 jit_solution(560110108480496360)
XLA Ops:
  8.2 3.8 %collective-permute-start = (bf16[3,1024]{0,1:T(8,128)(2,1)S(1)}, bf16[3,1024]{0,1:T(8,128)(2,1)S(1)}, u32[]{:S(2)}, u32[]{:S(2)}) collective-permute-start(bf16[3,1024]{0,1:T(8,128)(2,1)S(1)} %copy.76), channel_id=1, source_target_pairs={{0,8},{8,16},{16,24},{24,32},{32,40},{40,48},{48,56},{56,64},{64,7... | collective-permute-start | bytes 18440 | tf_op jit(solution)/shard_map/ppermute | solution.py:14
  12.7 3.8 %collective-permute-start.1 = (bf16[3,1,256]{2,0,1:T(4,128)(2,1)S(1)}, bf16[3,1,256]{2,0,1:T(4,128)(2,1)S(1)}, u32[]{:S(2)}, u32[]{:S(2)}) collective-permute-start(bf16[3,1,256]{2,0,1:T(4,128)(2,1)S(1)} %slice.125), channel_id=1, source_target_pairs={{0,8},{8,16},{16,24},{24,32},{32,40},{40,48},{48,56},{56,64},{64,7... | collective-permute-start | bytes 4616 | tf_op jit(solution)/shard_map/ppermute | solution.py:14
  24.3 1.5 fusion.96
  28.3 40.3 %all-gather = bf16[32,16,1]{1,2,0:T(2,128)(2,1)S(1)} all-gather(bf16[1,16,1]{1,2,0:T(2,128)(2,1)S(1)} %slice.213), channel_id=2, replica_groups=mesh['ctx'=32,'tp'=8] {'ctx'}, dimensions={0}, use_global_device_ids=true | all-gather | bytes 1056 | tf_op jit(solution)/shard_map/all_gather | solution.py:20
  71.8 54.2 %all-gather.10.cloned.1.call-done = bf16[512,64,128]{2,1,0:T(8,128)(2,1)} async-done(((bf16[16,64,128]{2,1,0:T(8,128)(2,1)}), bf16[512,64,128]{2,1,0:T(8,128)(2,1)}) %all-gather.10.cloned.1.call-update) | async-done | bytes 8388624 | tf_op jit(solution)/shard_map/all_gather | solution.py:20
  127.0 7.2 %convolution_convert_fusion = bf16[256,4096]{1,0:T(8,128)(2,1)} fusion(bf16[1024,4096]{1,0:T(8,128)(2,1)} %param.32, f32[256,1024]{0,1:T(8,128)S(1)} %get-tuple-element.171, f32[1024]{0:T(1024)S(1)} %copy-done, f32[256]{0:T(256)S(1)} %add_rsqrt_fusion), kind=kOutput, calls=%fused_computation.82 | convolution fusion | flops 2149318656 | bytes 11539456 | tf_op jit(solution)/shard_map/dot_general | solution.py:128
  137.2 66.5 %all-gather.6.cloned.1.call-done = bf16[8192,128]{1,0:T(8,128)(2,1)} async-done(((bf16[256,128]{1,0:T(8,128)(2,1)}), bf16[8192,128]{1,0:T(8,128)(2,1)}) %all-gather.6.cloned.1.call-update) | async-done | bytes 2097168 | tf_op jit(solution)/shard_map/all_gather | solution.py:140
  203.7 77.8 %all-gather.8.cloned.1.call-done = bf16[8192,128]{1,0:T(8,128)(2,1)} async-done(((bf16[256,128]{1,0:T(8,128)(2,1)}), bf16[8192,128]{1,0:T(8,128)(2,1)}) %all-gather.8.cloned.1.call-update) | async-done | bytes 2097168 | tf_op jit(solution)/shard_map/all_gather | solution.py:141
  281.5 15.4 %conditional.4 = (f32[1,8,64]{2,1,0:T(8,128)S(1)}, f32[1,8,64,128]{3,2,1,0:T(8,128)S(1)}) conditional(s32[]{:T(128)} %bitcast.73, () %tuple.48, (s32[8192]{0:T(1024)S(1)}, s32[256]{0:T(256)S(1)}, bf16[8192,1,128]{2,0,1:T(8,128)(2,1)}, bf16[256,1024]{1,0:T(8,128)(2,1)}, bf16[8192,1,128]{2,0,1:T(8,128)(2,1)}) %tuple.109), branch_computations={%region_6.7_spmd, %region_7.10_spmd} | conditional | flops 2202533376 | bytes 65450796 | solution.py:189
  281.8 4.8 %fusion = (f32[8,64]{1,0:T(8,128)S(1)}, f32[8192,64,8]{0,1,2:T(8,128)S(1)}) fusion(pred[64,8192]{1,0:T(8,128)(4,1)S(1)} %broadcast_compare_fusion, bf16[8192,1,128]{2,0,1:T(8,128)(2,1)} %get-tuple-element.97, bf16[256,1024]{1,0:T(8,128)(2,1)} %get-tuple-element.98), kind=kOutput, calls=%fused_computation.4 | convolution fusion | flops 1086324224 | bytes 19531776 | tf_op jit(solution)/shard_map/cond/branch_1_fun/bgrd,kgd->grbk/dot_general | solution.py:164
  286.7 4.7 %fusion.10 = f32[1,8,64,128]{3,2,1,0:T(8,128)S(1)} fusion(bf16[8192,1,128]{2,0,1:T(8,128)(2,1)S(1)} %copy-done.2, f32[8192,64,8]{0,1,2:T(8,128)S(1)} %get-tuple-element.179, f32[8,64]{1,0:T(8,128)S(1)} %broadcast_maximum_fusion, pred[64,8192]{1,0:T(8,128)(4,1)S(1)} %broadcast_compare_fusion), kind=kOutput, calls=%fused_computation.13 | convolution fusion | flops 1094713344 | bytes 19662848 | tf_op jit(solution)/shard_map/cond/branch_1_fun/grbk,kgd->grbd/dot_general | solution.py:177
  291.4 5.5 %fusion.2 = f32[8,64]{1,0:T(8,128)S(1)} fusion(f32[8192,64,8]{0,1,2:T(8,128)S(1)} %get-tuple-element.179, f32[8,64]{1,0:T(8,128)S(1)} %broadcast_maximum_fusion, pred[64,8192]{1,0:T(8,128)(4,1)S(1)} %broadcast_compare_fusion), kind=kLoop, calls=%fused_computation.6 | loop fusion | flops 20971008 | bytes 17305600 | tf_op jit(solution)/shard_map/cond/branch_1_fun/reduce_sum | solution.py:176
  296.9 15.5 %conditional.5 = (f32[1,8,64]{2,1,0:T(8,128)S(1)}, f32[1,8,64,128]{3,2,1,0:T(8,128)S(1)}) conditional(s32[]{:T(128)} %bitcast.76, () %tuple.50, (s32[8192]{0:T(1024)S(1)}, s32[256]{0:T(256)S(1)}, bf16[8192,1,128]{2,0,1:T(8,128)(2,1)}, bf16[256,1024]{1,0:T(8,128)(2,1)}, bf16[8192,1,128]{2,0,1:T(8,128)(2,1)}) %tuple.110), branch_computations={%region_10.11_spmd, %region_11.14_spmd} | conditional | flops 2202533376 | bytes 65450796 | solution.py:189
  297.3 4.9 %fusion.20 = (f32[8,64]{1,0:T(8,128)S(1)}, f32[8192,64,8]{0,1,2:T(8,128)S(1)}) fusion(pred[64,8192]{1,0:T(8,128)(4,1)S(1)} %broadcast_compare_fusion.1, bf16[8192,1,128]{2,0,1:T(8,128)(2,1)} %get-tuple-element.102, bf16[256,1024]{1,0:T(8,128)(2,1)} %get-tuple-element.103), kind=kOutput, calls=%fused_computation.24 | convolution fusion | flops 1086324224 | bytes 19531776 | tf_op jit(solution)/shard_map/cond/branch_1_fun/bgrd,kgd->grbk/dot_general | solution.py:164
  302.2 4.7 %fusion.30 = f32[1,8,64,128]{3,2,1,0:T(8,128)S(1)} fusion(bf16[8192,1,128]{2,0,1:T(8,128)(2,1)S(1)} %copy-done.3, f32[8192,64,8]{0,1,2:T(8,128)S(1)} %get-tuple-element.181, f32[8,64]{1,0:T(8,128)S(1)} %broadcast_maximum_fusion.1, pred[64,8192]{1,0:T(8,128)(4,1)S(1)} %broadcast_compare_fusion.1), kind=kOutput, calls=%fused_computation.33 | convolution fusion | flops 1094713344 | bytes 19662848 | tf_op jit(solution)/shard_map/cond/branch_1_fun/grbk,kgd->grbd/dot_general | solution.py:177
  306.9 5.5 %fusion.22 = f32[8,64]{1,0:T(8,128)S(1)} fusion(f32[8192,64,8]{0,1,2:T(8,128)S(1)} %get-tuple-element.181, f32[8,64]{1,0:T(8,128)S(1)} %broadcast_maximum_fusion.1, pred[64,8192]{1,0:T(8,128)(4,1)S(1)} %broadcast_compare_fusion.1), kind=kLoop, calls=%fused_computation.26 | loop fusion | flops 20971008 | bytes 17305600 | tf_op jit(solution)/shard_map/cond/branch_1_fun/reduce_sum | solution.py:176
  312.4 15.8 %conditional.6 = (f32[1,8,64]{2,1,0:T(8,128)S(1)}, f32[1,8,64,128]{3,2,1,0:T(8,128)S(1)}) conditional(s32[]{:T(128)} %bitcast.77, () %tuple.51, (s32[8192]{0:T(1024)S(1)}, s32[256]{0:T(256)S(1)}, bf16[8192,1,128]{2,0,1:T(8,128)(2,1)}, bf16[256,1024]{1,0:T(8,128)(2,1)}, bf16[8192,1,128]{2,0,1:T(8,128)(2,1)}) %tuple.111), branch_computations={%region_14.15_spmd, %region_15.18_spmd} | conditional | flops 2202533376 | bytes 65450796 | solution.py:189
  312.9 4.9 %fusion.40 = (f32[8,64]{1,0:T(8,128)S(1)}, f32[8192,64,8]{0,1,2:T(8,128)S(1)}) fusion(pred[64,8192]{1,0:T(8,128)(4,1)S(1)} %broadcast_compare_fusion.2, bf16[8192,1,128]{2,0,1:T(8,128)(2,1)} %get-tuple-element.107, bf16[256,1024]{1,0:T(8,128)(2,1)} %get-tuple-element.108), kind=kOutput, calls=%fused_computation.44 | convolution fusion | flops 1086324224 | bytes 19531776 | tf_op jit(solution)/shard_map/cond/branch_1_fun/bgrd,kgd->grbk/dot_general | solution.py:164
  317.8 4.8 %fusion.50 = f32[1,8,64,128]{3,2,1,0:T(8,128)S(1)} fusion(bf16[8192,1,128]{2,0,1:T(8,128)(2,1)S(1)} %copy-done.4, f32[8192,64,8]{0,1,2:T(8,128)S(1)} %get-tuple-element.183, f32[8,64]{1,0:T(8,128)S(1)} %broadcast_maximum_fusion.2, pred[64,8192]{1,0:T(8,128)(4,1)S(1)} %broadcast_compare_fusion.2), kind=kOutput, calls=%fused_computation.53 | convolution fusion | flops 1094713344 | bytes 19662848 | tf_op jit(solution)/shard_map/cond/branch_1_fun/grbk,kgd->grbd/dot_general | solution.py:177
  322.7 5.5 %fusion.42 = f32[8,64]{1,0:T(8,128)S(1)} fusion(f32[8192,64,8]{0,1,2:T(8,128)S(1)} %get-tuple-element.183, f32[8,64]{1,0:T(8,128)S(1)} %broadcast_maximum_fusion.2, pred[64,8192]{1,0:T(8,128)(4,1)S(1)} %broadcast_compare_fusion.2), kind=kLoop, calls=%fused_computation.46 | loop fusion | flops 20971008 | bytes 17305600 | tf_op jit(solution)/shard_map/cond/branch_1_fun/reduce_sum | solution.py:176
  328.1 15.5 %conditional.7 = (f32[1,8,64]{2,1,0:T(8,128)S(1)}, f32[1,8,64,128]{3,2,1,0:T(8,128)S(1)}) conditional(s32[]{:T(128)} %bitcast.78, () %tuple.52, (s32[8192]{0:T(1024)S(1)}, s32[256]{0:T(256)S(1)}, bf16[8192,1,128]{2,0,1:T(8,128)(2,1)}, bf16[256,1024]{1,0:T(8,128)(2,1)}, bf16[8192,1,128]{2,0,1:T(8,128)(2,1)}) %tuple.112), branch_computations={%region_18.19_spmd, %region_19.22_spmd} | conditional | flops 2202533376 | bytes 65450796 | solution.py:189
  328.6 4.9 %fusion.60 = (f32[8,64]{1,0:T(8,128)S(1)}, f32[8192,64,8]{0,1,2:T(8,128)S(1)}) fusion(pred[64,8192]{1,0:T(8,128)(4,1)S(1)} %broadcast_compare_fusion.3, bf16[8192,1,128]{2,0,1:T(8,128)(2,1)} %get-tuple-element.112, bf16[256,1024]{1,0:T(8,128)(2,1)} %get-tuple-element.113), kind=kOutput, calls=%fused_computation.64 | convolution fusion | flops 1086324224 | bytes 19531776 | tf_op jit(solution)/shard_map/cond/branch_1_fun/bgrd,kgd->grbk/dot_general | solution.py:164
  333.5 4.7 %fusion.70 = f32[1,8,64,128]{3,2,1,0:T(8,128)S(1)} fusion(bf16[8192,1,128]{2,0,1:T(8,128)(2,1)S(1)} %copy-done.5, f32[8192,64,8]{0,1,2:T(8,128)S(1)} %get-tuple-element.185, f32[8,64]{1,0:T(8,128)S(1)} %broadcast_maximum_fusion.3, pred[64,8192]{1,0:T(8,128)(4,1)S(1)} %broadcast_compare_fusion.3), kind=kOutput, calls=%fused_computation.73 | convolution fusion | flops 1094713344 | bytes 19662848 | tf_op jit(solution)/shard_map/cond/branch_1_fun/grbk,kgd->grbd/dot_general | solution.py:177
  338.1 5.5 %fusion.62 = f32[8,64]{1,0:T(8,128)S(1)} fusion(f32[8192,64,8]{0,1,2:T(8,128)S(1)} %get-tuple-element.185, f32[8,64]{1,0:T(8,128)S(1)} %broadcast_maximum_fusion.3, pred[64,8192]{1,0:T(8,128)(4,1)S(1)} %broadcast_compare_fusion.3), kind=kLoop, calls=%fused_computation.66 | loop fusion | flops 20971008 | bytes 17305600 | tf_op jit(solution)/shard_map/cond/branch_1_fun/reduce_sum | solution.py:176
  (79 shorter events, 19.8 us)
Async XLA Ops:
  7.2 118.8 %copy-start.1 = (f32[16]{0:T(128)S(1)}, f32[16]{0:T(128)}, u32[]{:S(2)}) copy-start(f32[16]{0:T(128)} %param.28) | copy-start | bytes 196
  7.2 119.8 %copy-start = (f32[1024]{0:T(1024)S(1)}, f32[1024]{0:T(1024)}, u32[]{:S(2)}) copy-start(f32[1024]{0:T(1024)} %param.31) | copy-start | bytes 12292
  7.2 118.7 %all-gather.10.cloned.1.call-start = ((), (), s32[]{:S(2)}) async-start(), calls=%async_computation.4 | async-start | bytes 8650752 | tf_op jit(solution)/shard_map/all_gather | solution.py:20
  8.2 16.1 %collective-permute-start = (bf16[3,1024]{0,1:T(8,128)(2,1)S(1)}, bf16[3,1024]{0,1:T(8,128)(2,1)S(1)}, u32[]{:S(2)}, u32[]{:S(2)}) collective-permute-start(bf16[3,1024]{0,1:T(8,128)(2,1)S(1)} %copy.76), channel_id=1, source_target_pairs={{0,8},{8,16},{16,24},{24,32},{32,40},{40,48},{48,56},{56,64},{64,7... | collective-permute-start | bytes 18440 | tf_op jit(solution)/shard_map/ppermute | solution.py:14
  12.7 10.1 %collective-permute-start.1 = (bf16[3,1,256]{2,0,1:T(4,128)(2,1)S(1)}, bf16[3,1,256]{2,0,1:T(4,128)(2,1)S(1)}, u32[]{:S(2)}, u32[]{:S(2)}) collective-permute-start(bf16[3,1,256]{2,0,1:T(4,128)(2,1)S(1)} %slice.125), channel_id=1, source_target_pairs={{0,8},{8,16},{16,24},{24,32},{32,40},{40,48},{48,56},{56,64},{64,7... | collective-permute-start | bytes 4616 | tf_op jit(solution)/shard_map/ppermute | solution.py:14
  26.8 176.9 %all-gather.6.cloned.1.call-start = ((), (), s32[]{:S(2)}) async-start(), calls=%async_computation.2 | async-start | bytes 2162688 | tf_op jit(solution)/shard_map/all_gather | solution.py:140
  27.5 254.0 %all-gather.8.cloned.1.call-start = ((), (), s32[]{:S(2)}) async-start(), calls=%async_computation.3 | async-start | bytes 2162688 | tf_op jit(solution)/shard_map/all_gather | solution.py:141
  28.3 317.1 %reduce-scatter.2.cloned.1.call-start = ((), (), s32[]{:S(2)}) async-start(), calls=%async_computation.1 | async-start | bytes 2359296 | tf_op jit(solution)/shard_map/reduce_scatter | solution.py:127
  281.5 5.2 %copy-start.2 = (bf16[8192,1,128]{2,0,1:T(8,128)(2,1)S(1)}, bf16[8192,1,128]{2,0,1:T(8,128)(2,1)}, u32[]{:S(2)}) copy-start(bf16[8192,1,128]{2,0,1:T(8,128)(2,1)} %get-tuple-element.99) | copy-start | bytes 6291460 | tf_op jit(solution)/shard_map/cond
  296.9 5.3 %copy-start.3 = (bf16[8192,1,128]{2,0,1:T(8,128)(2,1)S(1)}, bf16[8192,1,128]{2,0,1:T(8,128)(2,1)}, u32[]{:S(2)}) copy-start(bf16[8192,1,128]{2,0,1:T(8,128)(2,1)} %get-tuple-element.104) | copy-start | bytes 6291460 | tf_op jit(solution)/shard_map/cond
  312.6 5.3 %copy-start.4 = (bf16[8192,1,128]{2,0,1:T(8,128)(2,1)S(1)}, bf16[8192,1,128]{2,0,1:T(8,128)(2,1)}, u32[]{:S(2)}) copy-start(bf16[8192,1,128]{2,0,1:T(8,128)(2,1)} %get-tuple-element.109) | copy-start | bytes 6291460 | tf_op jit(solution)/shard_map/cond
  328.1 5.3 %copy-start.5 = (bf16[8192,1,128]{2,0,1:T(8,128)(2,1)S(1)}, bf16[8192,1,128]{2,0,1:T(8,128)(2,1)}, u32[]{:S(2)}) copy-start(bf16[8192,1,128]{2,0,1:T(8,128)(2,1)} %get-tuple-element.114) | copy-start | bytes 6291460 | tf_op jit(solution)/shard_map/cond
Sparse Core Ops, SparseCore 0:
  26.9 98.9 all-gather.9
  128.5 75.1 all-gather.5
  206.3 75.1 all-gather.7
  284.5 28.6 reduce-scatter.1
where the time goes:
time: 353 us; the launch traced here: 352 us
  waiting for transfers between devices  200 us (57%)
  matrix products  48.7 us (14%)
  blocking collectives  40.3 us (11%)
  other arithmetic  31.6 us (9%)
  between operations  16.4 us (5%)
  starting transfers between devices  7.79 us (2%)
  local copies, waits for them, and re-layouts  6.81 us (2%)
    all_gather x1, waiting for transfers between devices, per_device(): value_block = lax.all_gather(values, 'ctx', axis=0, tiled=True)  77.8 us
    all_gather x1, waiting for transfers between devices, per_device(): key_block = lax.all_gather(attention_keys, 'ctx', axis=0, tiled=True)  66.5 us
    all_gather x1, waiting for transfers between devices, prefix_2(): lax.all_gather(a.astype(kind), axis)  54.2 us
    all_gather x1, blocking collectives, prefix_2(): lax.all_gather(a.astype(kind), axis)  40.3 us
    reduce_sum x4, other arithmetic, update(): new_total = jnp.sum(weights, axis=3)  21.9 us
    dot_general x4, matrix products, update(): jnp.einsum('bgrd,kgd->grbk', query_tile_block, key_head_rows, preferred_e...  19.5 us
    dot_general x4, matrix products, update(): jnp.einsum('grbk,kgd->grbd', weights.astype(jnp.bfloat16), value_head_row...  18.8 us
    ppermute x2, starting transfers between devices, passed_along(): return lax.ppermute(shard, axis, pairs)  7.64 us
  transfers between devices with their start and end apart: 6, of which 3 were waited for; matrix products, arithmetic and copies ran while one was open for 24% of the time, Pallas kernels for 0%

commit v1 on v0

v1 whole, which is shorter than its diff:
```python
import functools

import jax
import jax.numpy as jnp
from jax import lax
from jax.experimental import pallas as pl
from jax.experimental.pallas import tpu as pltpu
from jax.sharding import PartitionSpec as P

F32 = jnp.float32
BF16 = jnp.bfloat16

TOK = 256
CH = 1024
HEADS = 16
NS = 128
NY, NZ = 4, 8
NX, NC = 4, 2
PART = 32
PACK = 48
QH = 8
HD = 128
DOUT = 4096
LOG2E = 1.4426950408889634


def dot_tt(a, b):
    return lax.dot_general(a, b, (((1,), (1,)), ((), ())), preferred_element_type=F32)


def lane_pair(lane, left, right):
    return jnp.where(lane < 64, left, right)


def sigmoid(x):
    return 1.0 / (1.0 + jnp.exp(-x))


def local_kernel(halo, xs, maps, taps_x, taps_m, steps, rates, pack, xc, bc, cols, rows, ext):
    ext[0:8, :] = halo[...].astype(F32)
    ext[8 : 8 + TOK, 0:CH] = xs[...].astype(F32)
    ext[8 : 8 + TOK, CH : CH + 256] = maps[...].astype(F32)
    weights_x = taps_x[...].astype(F32)
    weights_m = taps_m[...].astype(F32)

    def conv(lo, width, w):
        total = w[0:1] * ext[5 : 5 + TOK, lo : lo + width]
        for k in range(1, 4):
            total = total + w[k : k + 1] * ext[5 + k : 5 + k + TOK, lo : lo + width]
        return (total * sigmoid(total)).astype(BF16)

    bc[...] = conv(CH, 256, weights_m)
    dt = jax.nn.softplus(steps[...])
    eye = lax.broadcasted_iota(jnp.int32, (HEADS, HEADS), 0) == lax.broadcasted_iota(
        jnp.int32, (HEADS, HEADS), 1
    )
    rate_row = -jnp.exp(rates[...])
    rate = jnp.sum(
        jnp.where(eye, jnp.broadcast_to(rate_row, (HEADS, HEADS)), 0.0), axis=1, keepdims=True
    )
    cum = dt * rate
    token = lax.broadcasted_iota(jnp.int32, (HEADS, TOK), 1)
    for s in (1, 2, 4, 8, 16, 32, 64, 128):
        cum = cum + jnp.where(token >= s, pltpu.roll(cum, s, 1), 0.0)
    total = cum[:, TOK - 1 : TOK]
    tail = jnp.exp(total - cum) * dt
    rows[0:HEADS, :] = cum
    rows[HEADS : 2 * HEADS, :] = dt
    stacked = jnp.concatenate(
        [tail, cum, jnp.exp(cum), jnp.zeros((128 - 3 * HEADS, TOK), F32)], axis=0
    )
    columns = jnp.transpose(stacked)
    cols[...] = columns
    lane = lax.broadcasted_iota(jnp.int32, (TOK, 128), 1)
    b = bc[:, 0:NS]
    for j in range(8):
        lo = 128 * j
        x = conv(lo, 128, weights_x[:, lo : lo + 128])
        xc[:, lo : lo + 128] = x
        tail_pair = lane_pair(lane, columns[:, 2 * j : 2 * j + 1], columns[:, 2 * j + 1 : 2 * j + 2])
        weighted = (tail_pair * x.astype(F32)).astype(BF16)
        state = lax.dot_general(
            weighted, b, (((0,), (0,)), ((), ())), preferred_element_type=F32
        )
        pack[4 * j : 4 * j + 4, 0:PART, :] = state.astype(BF16).reshape(4, PART, NS)
    row = lax.broadcasted_iota(jnp.int32, (PACK - PART, NS), 0)
    hi = total.astype(BF16).astype(F32)
    mid = (total - hi).astype(BF16).astype(F32)
    low = total - hi - mid
    for h in range(HEADS):
        piece = jnp.where(
            row == 0,
            hi[h : h + 1, :],
            jnp.where(row == 1, mid[h : h + 1, :], jnp.where(row == 2, low[h : h + 1, :], 0.0)),
        ).astype(BF16)
        pack[2 * h, PART:PACK, :] = piece
        pack[2 * h + 1, PART:PACK, :] = piece


def local_part(halo, xs, maps, taps_x, taps_m, steps, rates):
    return pl.pallas_call(
        local_kernel,
        out_shape=(
            jax.ShapeDtypeStruct((32, PACK, NS), BF16),
            jax.ShapeDtypeStruct((TOK, CH), BF16),
            jax.ShapeDtypeStruct((TOK, 256), BF16),
            jax.ShapeDtypeStruct((TOK, 128), F32),
            jax.ShapeDtypeStruct((2 * HEADS, TOK), F32),
        ),
        scratch_shapes=[pltpu.VMEM((TOK + 8, CH + 256), F32)],
        name="mixer_local",
    )(halo, xs, maps, taps_x, taps_m, steps, rates)


def scan_kernel(got, out):
    entering = jnp.zeros((PART, NS), F32)
    for b in range(NY * NZ):
        out[b] = entering.astype(BF16)
        block = got[b].astype(F32)
        log_decay = block[PART : PART + 1] + block[PART + 1 : PART + 2] + block[PART + 2 : PART + 3]
        entering = jnp.exp(log_decay) * entering + block[0:PART]


def scan_part(got):
    return pl.pallas_call(
        scan_kernel, out_shape=jax.ShapeDtypeStruct((32, PART, NS), BF16), name="mixer_scan"
    )(got)


def inner_kernel(skip, xc, bc, cols, rows, out):
    g = dot_tt(bc[:, NS : 2 * NS], bc[:, 0:NS])
    t = lax.broadcasted_iota(jnp.int32, (TOK, TOK), 0)
    s = lax.broadcasted_iota(jnp.int32, (TOK, TOK), 1)
    g = jnp.where(t >= s, g, 0.0)
    lane = lax.broadcasted_iota(jnp.int32, (TOK, 128), 1)
    for j in range(8):
        x = xc[:, 128 * j : 128 * j + 128]
        parts = []
        for h in (2 * j, 2 * j + 1):
            gap = cols[:, HEADS + h : HEADS + h + 1] - rows[h : h + 1, :]
            mix = g * jnp.exp(jnp.minimum(gap, 0.0)) * rows[HEADS + h : HEADS + h + 1, :]
            parts.append(jnp.dot(mix.astype(BF16), x, preferred_element_type=F32))
        gain = lane_pair(lane, skip[2 * j], skip[2 * j + 1])
        out[:, 128 * j : 128 * j + 128] = lane_pair(lane, parts[0], parts[1]) + gain * x.astype(F32)


def inner_part(skip, xc, bc, cols, rows):
    vm = pl.BlockSpec(memory_space=pltpu.VMEM)
    return pl.pallas_call(
        inner_kernel,
        out_shape=jax.ShapeDtypeStruct((TOK, CH), F32),
        in_specs=[pl.BlockSpec(memory_space=pltpu.SMEM), vm, vm, vm, vm],
        name="mixer_inner",
    )(skip, xc, bc, cols, rows)


def project_kernel(place, y0, bc, entering, cols, gates, gain, weight, keep, send, u_ref, normed):
    @pl.when(pl.program_id(0) == 0)
    def _():
        lane = lax.broadcasted_iota(jnp.int32, (TOK, 128), 1)
        c = bc[:, NS : 2 * NS]
        square = jnp.zeros((TOK, 128), F32)
        for j in range(8):
            lo = 128 * j
            carried = dot_tt(c, entering[lo : lo + 128, :])
            h = 2 * HEADS + 2 * j
            decay = lane_pair(lane, cols[:, h : h + 1], cols[:, h + 1 : h + 2])
            y = y0[:, lo : lo + 128] + decay * carried
            z = gates[:, lo : lo + 128].astype(F32)
            u = y * (z * sigmoid(z))
            u_ref[:, lo : lo + 128] = u
            square = square + u * u
        mean = jnp.sum(square, axis=1, keepdims=True) * (1.0 / CH)
        scale = lax.rsqrt(mean + 1e-05)
        core = place[0]
        for d in range(NX * NC):
            first = 32 * (d // NC) + 128 * jnp.where(core == d % NC, 0, 1)
            first = pl.multiple_of(first, 32)
            value = u_ref[32 * d : 32 * d + 32, :] * scale[32 * d : 32 * d + 32] * gain[...]
            normed[pl.ds(first, 32), :] = value.astype(BF16)

    product = jnp.dot(normed[...], weight[...], preferred_element_type=F32).astype(BF16)
    keep[...] = product[0:128]
    send[...] = product[128:256]


def project_part(place, y0, bc, entering, cols, gates, gain, weight):
    block = 512
    whole = lambda *shape: pl.BlockSpec(shape, lambda i, p: (0,) * len(shape))
    half = jax.ShapeDtypeStruct((128, DOUT), BF16)
    return pl.pallas_call(
        project_kernel,
        out_shape=(half, half),
        grid_spec=pltpu.PrefetchScalarGridSpec(
            num_scalar_prefetch=1,
            grid=(DOUT // block,),
            in_specs=[
                whole(TOK, CH),
                whole(TOK, 256),
                whole(CH, NS),
                whole(TOK, 128),
                whole(TOK, CH),
                whole(1, CH),
                pl.BlockSpec((CH, block), lambda i, p: (0, i)),
            ],
            out_specs=[pl.BlockSpec((128, block), lambda i, p: (0, i))] * 2,
            scratch_shapes=[pltpu.VMEM((TOK, CH), F32), pltpu.VMEM((TOK, CH), BF16)],
        ),
        name="mixer_project",
    )(place, y0, bc, entering, cols, gates, gain, weight)


def pair_sum_kernel(place, keep, got, *outs):
    x = place[1]
    for s in range(NX):
        first = pl.multiple_of(((x + s) % NX) * 32, 32)
        total = keep[pl.ds(first, 32), :].astype(F32) + got[pl.ds(first, 32), :].astype(F32)
        outs[s][...] = total.astype(BF16)


def pair_sum(place, keep, got):
    vm = pl.BlockSpec(memory_space=pltpu.VMEM)
    return pl.pallas_call(
        pair_sum_kernel,
        out_shape=(jax.ShapeDtypeStruct((32, DOUT), BF16),) * NX,
        in_specs=[pl.BlockSpec(memory_space=pltpu.SMEM), vm, vm],
        name="pair_sum",
    )(place, keep, got)


def accumulate(q, k, v, state, allowed=None):
    peak, acc = state
    ones = jnp.ones(v.shape, BF16)
    scores = dot_tt(q, k) * (HD**-0.5 * LOG2E)
    if allowed is not None:
        scores = jnp.where(allowed, scores, -1e30)
    new_peak = jnp.maximum(peak, jnp.max(scores, axis=1, keepdims=True))
    weights = jnp.exp2(scores - new_peak).astype(BF16)
    acc = acc * jnp.exp2(peak - new_peak) + jnp.dot(
        weights, jnp.concatenate([v, ones], axis=1), preferred_element_type=F32
    )
    return new_peak, acc


def own_row_kernel(place, q, *refs):
    pieces, (peak_out, acc_out) = refs[:NZ], refs[NZ:]
    z = place[2]
    t = lax.broadcasted_iota(jnp.int32, (TOK, TOK), 0)
    s = lax.broadcasted_iota(jnp.int32, (TOK, TOK), 1)
    qv = q[...]
    own = pieces[0]
    state = (jnp.full((TOK, 1), -1e30, F32), jnp.zeros((TOK, 2 * HD), F32))
    peak, acc = accumulate(qv, own[0:TOK, :], own[TOK : 2 * TOK, :], state, t >= s)
    peak_out[0] = jnp.broadcast_to(peak, (TOK, HD))
    acc_out[0] = acc
    for o in range(1, NZ):

        @pl.when(o <= z)
        def _(piece=pieces[o]):
            peak, acc = accumulate(
                qv, piece[0:TOK, :], piece[TOK : 2 * TOK, :], (peak_out[0, :, 0:1], acc_out[0])
            )
            peak_out[0] = jnp.broadcast_to(peak, (TOK, HD))
            acc_out[0] = acc


STATE = (
    jax.ShapeDtypeStruct((QH, TOK, HD), F32),
    jax.ShapeDtypeStruct((QH, TOK, 2 * HD), F32),
)
STATE_SPECS = [
    pl.BlockSpec((1, TOK, HD), lambda h, p: (h, 0, 0)),
    pl.BlockSpec((1, TOK, 2 * HD), lambda h, p: (h, 0, 0)),
]


def whole_spec(a):
    return pl.BlockSpec(a.shape, lambda h, p: (0,) * a.ndim)


def own_row(place, q, pieces):
    return pl.pallas_call(
        own_row_kernel,
        out_shape=STATE,
        grid_spec=pltpu.PrefetchScalarGridSpec(
            num_scalar_prefetch=1,
            grid=(QH,),
            in_specs=[pl.BlockSpec((TOK, HD), lambda h, p: (0, h))] + [whole_spec(a) for a in pieces],
            out_specs=STATE_SPECS,
        ),
        name="attend_row",
    )(place, q, *pieces)


def rows_kernel(least, final, place, q, *refs):
    n = len(least)
    sets, (peak_in, acc_in), outs = refs[:n], refs[n : n + 2], refs[n + 2 :]
    y = place[3]
    scratch = outs[1:] if final else outs
    peak_out, acc_out = scratch
    peak_out[0] = peak_in[0]
    acc_out[0] = acc_in[0]
    qv = q[...]
    for low, ref in zip(least, sets):

        @pl.when(y >= low)
        def _(ref=ref):
            peak, acc = peak_out[0, :, 0:1], acc_out[0]
            for o in range(0, ref.shape[0], 2):
                k = jnp.concatenate([ref[o, 0:TOK, :], ref[o + 1, 0:TOK, :]], axis=0)
                v = jnp.concatenate([ref[o, TOK : 2 * TOK, :], ref[o + 1, TOK : 2 * TOK, :]], axis=0)
                peak, acc = accumulate(qv, k, v, (peak, acc))
            peak_out[0] = jnp.broadcast_to(peak, (TOK, HD))
            acc_out[0] = acc

    if final:
        acc = acc_out[0]
        outs[0][...] = (acc[:, 0:HD] / acc[:, HD : 2 * HD]).astype(BF16)


def other_rows(place, q, sets, least, state, final):
    specs = [pl.BlockSpec((TOK, HD), lambda h, p: (0, h))] + [whole_spec(a) for a in sets] + STATE_SPECS
    if final:
        out_shape = jax.ShapeDtypeStruct((TOK, QH * HD), BF16)
        out_specs = pl.BlockSpec((TOK, HD), lambda h, p: (0, h))
        scratch = [pltpu.VMEM((1, TOK, HD), F32), pltpu.VMEM((1, TOK, 2 * HD), F32)]
    else:
        out_shape, out_specs, scratch = STATE, STATE_SPECS, []
    return pl.pallas_call(
        functools.partial(rows_kernel, least, final),
        out_shape=out_shape,
        grid_spec=pltpu.PrefetchScalarGridSpec(
            num_scalar_prefetch=1,
            grid=(QH,),
            in_specs=specs,
            out_specs=out_specs,
            scratch_shapes=scratch,
        ),
        name="attend_rows",
    )(place, q, *sets, *state)


def along_z(step):
    return [(y * NZ + z, y * NZ + (z + step) % NZ) for y in range(NY) for z in range(NZ)]


def along_y(pairs):
    return [(a * NZ + z, b * NZ + z) for a, b in pairs for z in range(NZ)]


def along_x(step):
    return [(x * NC + c, ((x + step) % NX) * NC + c) for x in range(NX) for c in range(NC)]


def per_device(
    ssm_inputs,
    state_maps,
    ssm_gates,
    time_steps,
    log_rates,
    skip_gain,
    conv_inputs,
    conv_maps,
    norm_gain,
    out_weight,
    queries,
    attention_keys,
    values,
):
    ctx = lax.axis_index("ctx")
    tp = lax.axis_index("tp")
    place = jnp.stack([tp % NC, tp // NC, ctx % NZ, ctx // NZ]).astype(jnp.int32)
    maps = state_maps.reshape(TOK, 256)
    taps_m = conv_maps.reshape(4, 256)

    edge = jnp.concatenate([ssm_inputs[TOK - 8 :], maps[TOK - 8 :]], axis=1)
    halo = lax.ppermute(edge, "ctx", [(i, i + 1) for i in range(NY * NZ - 1)])
    kv = jnp.concatenate([attention_keys, values], axis=0)
    f1 = lax.ppermute(kv, "ctx", along_z(1))
    b1 = lax.ppermute(kv, "ctx", along_z(-1))
    pack, xc, bc, cols, rows = local_part(
        halo, ssm_inputs, maps, conv_inputs, taps_m, time_steps, log_rates.reshape(1, HEADS)
    )
    f2 = lax.ppermute(f1, "ctx", along_z(1))
    b2 = lax.ppermute(b1, "ctx", along_z(-1))
    got = lax.all_to_all(pack, "ctx", 0, 0)
    f3 = lax.ppermute(f2, "ctx", along_z(1))
    b3 = lax.ppermute(b2, "ctx", along_z(-1))
    f4 = lax.ppermute(f3, "ctx", along_z(1))
    y0 = inner_part(skip_gain, xc, bc, cols, rows)
    entering = lax.all_to_all(scan_part(got), "ctx", 0, 0).reshape(CH, NS)

    pieces = [kv, f1, f2, f3, f4, b3, b2, b1]
    row = jnp.stack(pieces)
    yf = lax.ppermute(row, "ctx", along_y([(0, 1), (1, 2), (2, 3)]))
    yb = lax.ppermute(row, "ctx", along_y([(0, 3), (1, 0)]))
    y2f = lax.ppermute(yf[: NZ // 2], "ctx", along_y([(1, 2), (2, 3)]))
    y2b = lax.ppermute(yb[NZ // 2 :], "ctx", along_y([(3, 2), (0, 3)]))
    state = own_row(place, queries, pieces)
    state = other_rows(place, queries, [yf, yb], [1, 3], state, False)

    keep, send = project_part(
        place, y0, bc, entering, cols, ssm_gates, norm_gain.reshape(1, CH), out_weight
    )
    swapped = lax.ppermute(send, "tp", [(i, i ^ 1) for i in range(NX * NC)])
    sums = pair_sum(place, keep, swapped)
    others = [lax.ppermute(sums[s], "tp", along_x(s)) for s in range(1, NX)]
    total = sums[0].astype(F32)
    for a in others:
        total = total + a.astype(F32)
    ssm_out = total.astype(BF16)

    attn_out = other_rows(place, queries, [y2f, y2b], [2, 2], state, True)
    return ssm_out, attn_out


def solution(mesh):
    placed = (
        P("ctx", "tp"),
        P("ctx", "tp", None),
        P("ctx", "tp"),
        P("tp", "ctx"),
        P("tp"),
        P("tp"),
        P(None, "tp"),
        P(None, "tp", None),
        P("tp"),
        P("tp", None),
        P("ctx", "tp"),
        P("ctx", "tp"),
        P("ctx", "tp"),
    )
    return jax.shard_map(
        per_device,
        mesh=mesh,
        in_specs=placed,
        out_specs=(P(("ctx", "tp"), None), P("ctx", "tp")),
        check_vma=False,
    )
```

time: 353 us -> 186 us (0.53)
  the two profiles are of different devices: /device:TPU:4 before, /device:TPU:248 now
where the time goes in v1:
time: 186 us; the launch traced here: 185 us
  Pallas kernels  100 us (54%)
  starting transfers between devices  45.9 us (25%)
  waiting for transfers between devices  23 us (12%)
  local copies, waits for them, and re-layouts  13.3 us (7%)
    pallas_call x2, Pallas kernels, other_rows(): pl.pallas_call(functools.partial(rows_kernel, least, final), out_shape=ou...  40.5 us
    pallas_call x1, Pallas kernels, own_row(): pl.pallas_call(own_row_kernel, out_shape=STATE, grid_spec=pltpu.PrefetchS...  36.4 us
    all_to_all x1, starting transfers between devices, per_device(): got = lax.all_to_all(pack, 'ctx', 0, 0)  10.8 us
    all_to_all x1, starting transfers between devices, per_device(): entering = lax.all_to_all(scan_part(got), 'ctx', 0, 0).reshape(CH, NS)  10.6 us
    pallas_call x1, Pallas kernels, project_part(): pl.pallas_call(project_kernel, out_shape=(half, half), grid_spec=pltpu.Pr...  10.6 us
    unnamed x38, local copies, waits for them, and re-layouts  8.61 us
    ppermute x1, waiting for transfers between devices, per_device(): f2 = lax.ppermute(f1, 'ctx', along_z(1))  8.29 us
    ppermute x1, waiting for transfers between devices, per_device(): yf = lax.ppermute(row, 'ctx', along_y([(0, 1), (1, 2), (2, 3)]))  6.2 us
  transfers between devices with their start and end apart: 18, of which 5 were waited for; matrix products, arithmetic and copies ran while one was open for 5% of the time, Pallas kernels for 53%

profile of v1, /device:TPU:248, one launch (start us, length us, event | category | flops | bytes accessed | tf_op | source)
XLA Modules:
  0.0 184.8 jit_solution(2803335758192288962)
XLA Ops:
  2.4 2.0 %collective-permute-start.9 = (bf16[512,128]{1,0:T(8,128)(2,1)S(1)}, bf16[512,128]{1,0:T(8,128)(2,1)S(1)}, u32[]{:S(2)}, u32[]{:S(2)}) collective-permute-start(bf16[512,128]{1,0:T(8,128)(2,1)S(1)} %constant_dynamic-update-slice_fusion.refs_0_), channel_id=1, source_target_pairs={{0,56},{8,0},{16,8},{24,16},{32,24},{40,32},{48,40},{56,48},{64,12... | collective-permute-start | bytes 393224 | tf_op jit(solution)/shard_map/ppermute | solution.py:380
  7.8 3.7 %collective-permute-done.halo = bf16[8,1280]{1,0:T(8,128)(2,1)S(1)} collective-permute-done((bf16[8,1280]{1,0:T(8,128)(2,1)S(1)}, bf16[8,1280]{1,0:T(8,128)(2,1)S(1)}, u32[]{:S(2)}, u32[]{:S(2)}) %collective-permute-start) | collective-permute-done | bytes 20512 | tf_op jit(solution)/shard_map/ppermute | solution.py:377
  12.1 4.7 %mixer_local.1 = (bf16[32,48,128]{2,1,0:T(8,128)(2,1)}, bf16[256,1024]{1,0:T(8,128)(2,1)}, bf16[256,256]{1,0:T(8,128)(2,1)}, f32[256,128]{1,0:T(8,128)}, f32[32,256]{1,0:T(8,128)}) custom-call(bf16[8,1280]{1,0:T(8,128)(2,1)} %copy-done.14, bf16[256,1024]{1,0:T(8,128)(2,1)} %xs.1, bf16[256,256]{1,0:T(8,128)(2,1)} %bitcast.28, bf16[4,1024]{1,0:T(4,128)(2,1)} %taps_x.1, ...), custom_call_target="tpu_custom_call" | custom-call | tf_op jit(solution)/shard_map/mixer_local/pallas_call | solution.py:101
  16.8 10.8 %all-to-all-start = ((bf16[32,48,128]{2,1,0:T(8,128)(2,1)}), bf16[32,48,128]{2,1,0:T(8,128)(2,1)S(1)}, u32[]{:S(2)}, u32[]{:S(2)}) async-start(bf16[32,48,128]{2,1,0:T(8,128)(2,1)} %get-tuple-element.21), calls=%async_computation | async-start | bytes 786432 | tf_op jit(solution)/shard_map/all_to_all | solution.py:386
  28.2 1.5 collective-permute-start.10
  30.4 8.3 %collective-permute-done.6.refs_2_ = bf16[512,128]{1,0:T(8,128)(2,1)S(1)} collective-permute-done((bf16[512,128]{1,0:T(8,128)(2,1)S(1)}, bf16[512,128]{1,0:T(8,128)(2,1)S(1)}, u32[]{:S(2)}, u32[]{:S(2)}) %collective-permute-start.6) | collective-permute-done | bytes 131104 | tf_op jit(solution)/shard_map/ppermute | solution.py:384
  38.7 1.9 %collective-permute-start.7 = (bf16[512,128]{1,0:T(8,128)(2,1)S(1)}, bf16[512,128]{1,0:T(8,128)(2,1)S(1)}, u32[]{:S(2)}, u32[]{:S(2)}) collective-permute-start(bf16[512,128]{1,0:T(8,128)(2,1)S(1)} %collective-permute-done.6.refs_2_), channel_id=1, source_target_pairs={{0,8},{8,16},{16,24},{24,32},{32,40},{40,48},{48,56},{56,0},{64,72... | collective-permute-start | bytes 393224 | tf_op jit(solution)/shard_map/ppermute | solution.py:387
  41.4 2.9 %collective-permute-done.7.refs_3_ = bf16[512,128]{1,0:T(8,128)(2,1)S(1)} collective-permute-done((bf16[512,128]{1,0:T(8,128)(2,1)S(1)}, bf16[512,128]{1,0:T(8,128)(2,1)S(1)}, u32[]{:S(2)}, u32[]{:S(2)}) %collective-permute-start.7) | collective-permute-done | bytes 131104 | tf_op jit(solution)/shard_map/ppermute | solution.py:387
  44.2 2.6 %collective-permute-start.8 = (bf16[512,128]{1,0:T(8,128)(2,1)S(1)}, bf16[512,128]{1,0:T(8,128)(2,1)S(1)}, u32[]{:S(2)}, u32[]{:S(2)}) collective-permute-start(bf16[512,128]{1,0:T(8,128)(2,1)S(1)} %collective-permute-done.7.refs_3_), channel_id=1, source_target_pairs={{0,8},{8,16},{16,24},{24,32},{32,40},{40,48},{48,56},{56,0},{64,72... | collective-permute-start | bytes 393224 | tf_op jit(solution)/shard_map/ppermute | solution.py:389
  47.5 1.9 %collective-permute-done.8.refs_4_ = bf16[512,128]{1,0:T(8,128)(2,1)S(1)} collective-permute-done((bf16[512,128]{1,0:T(8,128)(2,1)S(1)}, bf16[512,128]{1,0:T(8,128)(2,1)S(1)}, u32[]{:S(2)}, u32[]{:S(2)}) %collective-permute-start.8) | collective-permute-done | bytes 131104 | tf_op jit(solution)/shard_map/ppermute | solution.py:389
  51.6 1.8 mixer_scan.1
  53.4 10.6 %all-to-all-start.1 = ((bf16[32,32,128]{2,1,0:T(8,128)(2,1)}), bf16[32,32,128]{2,1,0:T(8,128)(2,1)S(1)}, u32[]{:S(2)}, u32[]{:S(2)}) async-start(bf16[32,32,128]{2,1,0:T(8,128)(2,1)} %mixer_scan.1), calls=%async_computation.1 | async-start | bytes 524288 | tf_op jit(solution)/shard_map/all_to_all | solution.py:391
  66.6 1.3 collective-permute-start.14
  68.6 3.5 %mixer_inner.1.y0 = f32[256,1024]{1,0:T(8,128)} custom-call(f32[16]{0:T(128)} %skip.1, bf16[256,1024]{1,0:T(8,128)(2,1)} %get-tuple-element.17.xc, bf16[256,256]{1,0:T(8,128)(2,1)} %get-tuple-element.18.bc, f32[256,128]{1,0:T(8,128)} %get-tuple-element.19.cols, f32[32,256]{1,0:T(8,128)} %get-tuple-element.20.rows), custom_call_target="tpu_custom_call" | custom-call | tf_op jit(solution)/shard_map/mixer_inner/pallas_call | solution.py:149
  72.9 10.6 %mixer_project.1 = (bf16[128,4096]{1,0:T(8,128)(2,1)}, bf16[128,4096]{1,0:T(8,128)(2,1)}) custom-call(s32[4]{0:T(128)} %pad_add_fusion.place, f32[256,1024]{1,0:T(8,128)} %mixer_inner.1.y0, bf16[256,256]{1,0:T(8,128)(2,1)} %get-tuple-element.18.bc, bf16[1024,128]{1,0:T(8,128)(2,1)} %bitcast.27, f32[256,128]{1,0:T(8,128)} %get-tuple-element.19.cols, ...), custom_call_target="tpu_custom_call" | custom-call | tf_op jit(solution)/shard_map/mixer_project/pallas_call | solution.py:191
  83.7 6.2 %collective-permute-done.12.refs_0_ = bf16[8,512,128]{2,1,0:T(8,128)(2,1)S(1)} collective-permute-done((bf16[8,512,128]{2,1,0:T(8,128)(2,1)}, bf16[8,512,128]{2,1,0:T(8,128)(2,1)S(1)}, u32[]{:S(2)}, u32[]{:S(2)}) %collective-permute-start.12) | collective-permute-done | bytes 1048608 | tf_op jit(solution)/shard_map/ppermute | solution.py:395
  93.0 4.5 %collective-permute-start.15 = (bf16[4,512,128]{2,1,0:T(8,128)(2,1)}, bf16[4,512,128]{2,1,0:T(8,128)(2,1)}, u32[]{:S(2)}, u32[]{:S(2)}) collective-permute-start(bf16[4,512,128]{2,1,0:T(8,128)(2,1)} %slice.21), channel_id=1, source_target_pairs={{192,128},{200,136},{208,144},{216,152},{224,160},{232,168},{240,1... | collective-permute-start | bytes 1572872 | tf_op jit(solution)/shard_map/ppermute | solution.py:398
  98.6 2.7 %pair_sum.1 = (bf16[32,4096]{1,0:T(8,128)(2,1)}, bf16[32,4096]{1,0:T(8,128)(2,1)}, bf16[32,4096]{1,0:T(8,128)(2,1)}, bf16[32,4096]{1,0:T(8,128)(2,1)}) custom-call(s32[4]{0:T(128)} %pad_add_fusion.place, bf16[128,4096]{1,0:T(8,128)(2,1)} %get-tuple-element.22.keep, bf16[128,4096]{1,0:T(8,128)(2,1)} %copy-done.3), custom_call_target="tpu_custom_call" | custom-call | tf_op jit(solution)/shard_map/pair_sum/pallas_call | solution.py:223
  101.3 1.5 collective-permute-start.2
  102.8 2.7 %collective-permute-start.3 = (bf16[32,4096]{1,0:T(8,128)(2,1)}, bf16[32,4096]{1,0:T(8,128)(2,1)S(1)}, u32[]{:S(2)}, u32[]{:S(2)}) collective-permute-start(bf16[32,4096]{1,0:T(8,128)(2,1)} %get-tuple-element.26), channel_id=1, source_target_pairs={{0,4},{1,5},{2,6},{3,7},{4,0},{5,1},{6,2},{7,3},{8,12},{9,13},{10,... | collective-permute-start | bytes 786440 | tf_op jit(solution)/shard_map/ppermute | solution.py:407
  105.5 1.4 collective-permute-start.4
  106.9 36.4 %attend_row.1 = (f32[8,256,128]{2,1,0:T(8,128)}, f32[8,256,256]{2,1,0:T(8,128)}) custom-call(s32[4]{0:T(128)} %pad_add_fusion.place, bf16[256,1024]{1,0:T(8,128)(2,1)} %q.5, bf16[512,128]{1,0:T(8,128)(2,1)} %copy-done.5, bf16[512,128]{1,0:T(8,128)(2,1)} %copy-done.6, bf16[512,128]{1,0:T(8,128)(2,1)} %copy-done.8, bf16[512,128]{1,0:T(8,128)(2,1)} %copy-done.10, ...), custom_call_target="tpu_custom_call" | custom-call | tf_op jit(solution)/shard_map/attend_row/pallas_call | solution.py:282
  143.4 25.9 %attend_rows.2 = (f32[8,256,128]{2,1,0:T(8,128)}, f32[8,256,256]{2,1,0:T(8,128)}) custom-call(s32[4]{0:T(128)} %pad_add_fusion.place, bf16[256,1024]{1,0:T(8,128)(2,1)} %q.5, bf16[8,512,128]{2,1,0:T(8,128)(2,1)} %copy-done, bf16[8,512,128]{2,1,0:T(8,128)(2,1)} %copy-done.1, f32[8,256,128]{2,1,0:T(8,128)} %get-tuple-element.28.refs_2_, ...), custom_call_target="tpu_custom_call" | custom-call | tf_op jit(solution)/shard_map/attend_rows/pallas_call | solution.py:329
  169.3 14.6 %attend_rows.3 = bf16[256,1024]{1,0:T(8,128)(2,1)} custom-call(s32[4]{0:T(128)} %pad_add_fusion.place, bf16[256,1024]{1,0:T(8,128)(2,1)} %q.5, bf16[4,512,128]{2,1,0:T(8,128)(2,1)} %collective-permute-done.13.refs_0_, bf16[4,512,128]{2,1,0:T(8,128)(2,1)} %collective-permute-done.15.refs_1_, f32[8,256,128]{2,1,0:T(8,128)} %get-tuple-element.30.refs_2_, ...), custom_call_target="tpu_custom_call" | custom-call | tf_op jit(solution)/shard_map/attend_rows/pallas_call | solution.py:329
  (67 shorter events, 19.8 us)
Async XLA Ops:
  2.3 51.0 %copy-start.5 = (bf16[512,128]{1,0:T(8,128)(2,1)}, bf16[512,128]{1,0:T(8,128)(2,1)S(1)}, u32[]{:S(2)}) copy-start(bf16[512,128]{1,0:T(8,128)(2,1)S(1)} %constant_dynamic-update-slice_fusion.refs_0_) | copy-start | bytes 393220
  2.3 25.3 %collective-permute-start.5 = (bf16[512,128]{1,0:T(8,128)(2,1)S(1)}, bf16[512,128]{1,0:T(8,128)(2,1)S(1)}, u32[]{:S(2)}, u32[]{:S(2)}) collective-permute-start(bf16[512,128]{1,0:T(8,128)(2,1)S(1)} %constant_dynamic-update-slice_fusion.refs_0_), channel_id=1, source_target_pairs={{0,8},{8,16},{16,24},{24,32},{32,40},{40,48},{48,56},{56,0},{64,72... | collective-permute-start | bytes 393224 | tf_op jit(solution)/shard_map/ppermute | solution.py:379
  2.4 25.8 %collective-permute-start.9 = (bf16[512,128]{1,0:T(8,128)(2,1)S(1)}, bf16[512,128]{1,0:T(8,128)(2,1)S(1)}, u32[]{:S(2)}, u32[]{:S(2)}) collective-permute-start(bf16[512,128]{1,0:T(8,128)(2,1)S(1)} %constant_dynamic-update-slice_fusion.refs_0_), channel_id=1, source_target_pairs={{0,56},{8,0},{16,8},{24,16},{32,24},{40,32},{48,40},{56,48},{64,12... | collective-permute-start | bytes 393224 | tf_op jit(solution)/shard_map/ppermute | solution.py:380
  5.9 5.7 %collective-permute-start = (bf16[8,1280]{1,0:T(8,128)(2,1)S(1)}, bf16[8,1280]{1,0:T(8,128)(2,1)S(1)}, u32[]{:S(2)}, u32[]{:S(2)}) collective-permute-start(bf16[8,1280]{1,0:T(8,128)(2,1)S(1)} %pad_maximum_fusion), channel_id=1, source_target_pairs={{0,8},{8,16},{16,24},{24,32},{32,40},{40,48},{48,56},{56,64},{64,7... | collective-permute-start | bytes 61448 | tf_op jit(solution)/shard_map/ppermute | solution.py:377
  16.8 34.0 %all-to-all-start = ((bf16[32,48,128]{2,1,0:T(8,128)(2,1)}), bf16[32,48,128]{2,1,0:T(8,128)(2,1)S(1)}, u32[]{:S(2)}, u32[]{:S(2)}) async-start(bf16[32,48,128]{2,1,0:T(8,128)(2,1)} %get-tuple-element.21), calls=%async_computation | async-start | bytes 786432 | tf_op jit(solution)/shard_map/all_to_all | solution.py:386
  27.6 44.5 %copy-start.6 = (bf16[512,128]{1,0:T(8,128)(2,1)}, bf16[512,128]{1,0:T(8,128)(2,1)S(1)}, u32[]{:S(2)}) copy-start(bf16[512,128]{1,0:T(8,128)(2,1)S(1)} %collective-permute-done.5.refs_1_) | copy-start | bytes 393220
  27.6 11.1 %collective-permute-start.6 = (bf16[512,128]{1,0:T(8,128)(2,1)S(1)}, bf16[512,128]{1,0:T(8,128)(2,1)S(1)}, u32[]{:S(2)}, u32[]{:S(2)}) collective-permute-start(bf16[512,128]{1,0:T(8,128)(2,1)S(1)} %collective-permute-done.5.refs_1_), channel_id=1, source_target_pairs={{0,8},{8,16},{16,24},{24,32},{32,40},{40,48},{48,56},{56,0},{64,72... | collective-permute-start | bytes 393224 | tf_op jit(solution)/shard_map/ppermute | solution.py:384
  28.2 43.9 %copy-start.7 = (bf16[512,128]{1,0:T(8,128)(2,1)}, bf16[512,128]{1,0:T(8,128)(2,1)S(1)}, u32[]{:S(2)}) copy-start(bf16[512,128]{1,0:T(8,128)(2,1)S(1)} %collective-permute-done.9.refs_7_) | copy-start | bytes 393220
  28.2 12.3 %collective-permute-start.10 = (bf16[512,128]{1,0:T(8,128)(2,1)S(1)}, bf16[512,128]{1,0:T(8,128)(2,1)S(1)}, u32[]{:S(2)}, u32[]{:S(2)}) collective-permute-start(bf16[512,128]{1,0:T(8,128)(2,1)S(1)} %collective-permute-done.9.refs_7_), channel_id=1, source_target_pairs={{0,56},{8,0},{16,8},{24,16},{32,24},{40,32},{48,40},{56,48},{64,12... | collective-permute-start | bytes 393224 | tf_op jit(solution)/shard_map/ppermute | solution.py:385
  38.7 5.6 %collective-permute-start.7 = (bf16[512,128]{1,0:T(8,128)(2,1)S(1)}, bf16[512,128]{1,0:T(8,128)(2,1)S(1)}, u32[]{:S(2)}, u32[]{:S(2)}) collective-permute-start(bf16[512,128]{1,0:T(8,128)(2,1)S(1)} %collective-permute-done.6.refs_2_), channel_id=1, source_target_pairs={{0,8},{8,16},{16,24},{24,32},{32,40},{40,48},{48,56},{56,0},{64,72... | collective-permute-start | bytes 393224 | tf_op jit(solution)/shard_map/ppermute | solution.py:387
  40.5 31.6 %copy-start.9 = (bf16[512,128]{1,0:T(8,128)(2,1)}, bf16[512,128]{1,0:T(8,128)(2,1)S(1)}, u32[]{:S(2)}) copy-start(bf16[512,128]{1,0:T(8,128)(2,1)S(1)} %collective-permute-done.10.refs_6_) | copy-start | bytes 393220
  40.5 9.6 %collective-permute-start.11 = (bf16[512,128]{1,0:T(8,128)(2,1)S(1)}, bf16[512,128]{1,0:T(8,128)(2,1)S(1)}, u32[]{:S(2)}, u32[]{:S(2)}) collective-permute-start(bf16[512,128]{1,0:T(8,128)(2,1)S(1)} %collective-permute-done.10.refs_6_), channel_id=1, source_target_pairs={{0,56},{8,0},{16,8},{24,16},{32,24},{40,32},{48,40},{56,48},{64,12... | collective-permute-start | bytes 393224 | tf_op jit(solution)/shard_map/ppermute | solution.py:388
  44.2 5.1 %collective-permute-start.8 = (bf16[512,128]{1,0:T(8,128)(2,1)S(1)}, bf16[512,128]{1,0:T(8,128)(2,1)S(1)}, u32[]{:S(2)}, u32[]{:S(2)}) collective-permute-start(bf16[512,128]{1,0:T(8,128)(2,1)S(1)} %collective-permute-done.7.refs_3_), channel_id=1, source_target_pairs={{0,8},{8,16},{16,24},{24,32},{32,40},{40,48},{48,56},{56,0},{64,72... | collective-permute-start | bytes 393224 | tf_op jit(solution)/shard_map/ppermute | solution.py:389
  50.1 33.4 %copy-start.11 = (bf16[512,128]{1,0:T(8,128)(2,1)}, bf16[512,128]{1,0:T(8,128)(2,1)S(1)}, u32[]{:S(2)}) copy-start(bf16[512,128]{1,0:T(8,128)(2,1)S(1)} %collective-permute-done.11.refs_5_) | copy-start | bytes 393220
  53.4 18.8 %all-to-all-start.1 = ((bf16[32,32,128]{2,1,0:T(8,128)(2,1)}), bf16[32,32,128]{2,1,0:T(8,128)(2,1)S(1)}, u32[]{:S(2)}, u32[]{:S(2)}) async-start(bf16[32,32,128]{2,1,0:T(8,128)(2,1)} %mixer_scan.1), calls=%async_computation.1 | async-start | bytes 524288 | tf_op jit(solution)/shard_map/all_to_all | solution.py:391
  65.3 24.6 %collective-permute-start.12 = (bf16[8,512,128]{2,1,0:T(8,128)(2,1)}, bf16[8,512,128]{2,1,0:T(8,128)(2,1)S(1)}, u32[]{:S(2)}, u32[]{:S(2)}) collective-permute-start(bf16[8,512,128]{2,1,0:T(8,128)(2,1)} %bitcast_dynamic-update-slice_fusion), channel_id=1, source_target_pairs={{0,64},{8,72},{16,80},{24,88},{32,96},{40,104},{48,112},{56,120},{... | collective-permute-start | bytes 3145736 | tf_op jit(solution)/shard_map/ppermute | solution.py:395
  66.6 25.5 %collective-permute-start.14 = (bf16[8,512,128]{2,1,0:T(8,128)(2,1)}, bf16[8,512,128]{2,1,0:T(8,128)(2,1)S(1)}, u32[]{:S(2)}, u32[]{:S(2)}) collective-permute-start(bf16[8,512,128]{2,1,0:T(8,128)(2,1)} %bitcast_dynamic-update-slice_fusion), channel_id=1, source_target_pairs={{0,192},{8,200},{16,208},{24,216},{32,224},{40,232},{48,240},{56,2... | collective-permute-start | bytes 3145736 | tf_op jit(solution)/shard_map/ppermute | solution.py:396
  83.5 14.1 %collective-permute-start.1 = (bf16[128,4096]{1,0:T(8,128)(2,1)}, bf16[128,4096]{1,0:T(8,128)(2,1)S(1)}, u32[]{:S(2)}, u32[]{:S(2)}) collective-permute-start(bf16[128,4096]{1,0:T(8,128)(2,1)} %get-tuple-element.23), channel_id=1, source_target_pairs={{0,1},{1,0},{2,3},{3,2},{4,5},{5,4},{6,7},{7,6},{8,9},{9,8},{10,11... | collective-permute-start | bytes 3145736 | tf_op jit(solution)/shard_map/ppermute | solution.py:405
  90.9 78.4 %collective-permute-start.13 = (bf16[4,512,128]{2,1,0:T(8,128)(2,1)}, bf16[4,512,128]{2,1,0:T(8,128)(2,1)}, u32[]{:S(2)}, u32[]{:S(2)}) collective-permute-start(bf16[4,512,128]{2,1,0:T(8,128)(2,1)} %slice.20), channel_id=1, source_target_pairs={{64,128},{72,136},{80,144},{88,152},{96,160},{104,168},{112,176},{... | collective-permute-start | bytes 1572872 | tf_op jit(solution)/shard_map/ppermute | solution.py:397
  92.1 51.2 %copy-start.1 = (bf16[8,512,128]{2,1,0:T(8,128)(2,1)}, bf16[8,512,128]{2,1,0:T(8,128)(2,1)S(1)}, u32[]{:S(2)}) copy-start(bf16[8,512,128]{2,1,0:T(8,128)(2,1)S(1)} %collective-permute-done.14.refs_1_) | copy-start | bytes 3145732
  93.0 76.2 %collective-permute-start.15 = (bf16[4,512,128]{2,1,0:T(8,128)(2,1)}, bf16[4,512,128]{2,1,0:T(8,128)(2,1)}, u32[]{:S(2)}, u32[]{:S(2)}) collective-permute-start(bf16[4,512,128]{2,1,0:T(8,128)(2,1)} %slice.21), channel_id=1, source_target_pairs={{192,128},{200,136},{208,144},{216,152},{224,160},{232,168},{240,1... | collective-permute-start | bytes 1572872 | tf_op jit(solution)/shard_map/ppermute | solution.py:398
  101.3 82.7 %collective-permute-start.2 = (bf16[32,4096]{1,0:T(8,128)(2,1)}, bf16[32,4096]{1,0:T(8,128)(2,1)S(1)}, u32[]{:S(2)}, u32[]{:S(2)}) collective-permute-start(bf16[32,4096]{1,0:T(8,128)(2,1)} %get-tuple-element.25), channel_id=1, source_target_pairs={{0,2},{1,3},{2,4},{3,5},{4,6},{5,7},{6,0},{7,1},{8,10},{9,11},{10,... | collective-permute-start | bytes 786440 | tf_op jit(solution)/shard_map/ppermute | solution.py:407
  102.8 81.2 %collective-permute-start.3 = (bf16[32,4096]{1,0:T(8,128)(2,1)}, bf16[32,4096]{1,0:T(8,128)(2,1)S(1)}, u32[]{:S(2)}, u32[]{:S(2)}) collective-permute-start(bf16[32,4096]{1,0:T(8,128)(2,1)} %get-tuple-element.26), channel_id=1, source_target_pairs={{0,4},{1,5},{2,6},{3,7},{4,0},{5,1},{6,2},{7,3},{8,12},{9,13},{10,... | collective-permute-start | bytes 786440 | tf_op jit(solution)/shard_map/ppermute | solution.py:407
  105.5 78.4 %collective-permute-start.4 = (bf16[32,4096]{1,0:T(8,128)(2,1)}, bf16[32,4096]{1,0:T(8,128)(2,1)S(1)}, u32[]{:S(2)}, u32[]{:S(2)}) collective-permute-start(bf16[32,4096]{1,0:T(8,128)(2,1)} %get-tuple-element.27), channel_id=1, source_target_pairs={{0,6},{1,7},{2,0},{3,1},{4,2},{5,3},{6,4},{7,5},{8,14},{9,15},{10,... | collective-permute-start | bytes 786440 | tf_op jit(solution)/shard_map/ppermute | solution.py:407
  (9 other events, 106.3 us)

commit v2 on v1

v2 whole, which is shorter than its diff:
```python
import functools

import jax
import jax.numpy as jnp
from jax import lax
from jax.experimental import pallas as pl
from jax.experimental.pallas import tpu as pltpu
from jax.sharding import PartitionSpec as P


F32 = jnp.float32
BF16 = jnp.bfloat16

TOK = 256
CH = 1024
HEADS = 16
NS = 128
NY, NZ = 4, 8
NX, NC = 4, 2
PART = 32
PACK = 48
QH = 8
HD = 128
DOUT = 4096
LOG2E = 1.4426950408889634
PARAMS = pltpu.CompilerParams(vmem_limit_bytes=24 * 2**20)


def dot_tt(a, b):
    return lax.dot_general(a, b, (((1,), (1,)), ((), ())), preferred_element_type=F32)


def lane_pair(lane, left, right):
    return jnp.where(lane < 64, left, right)


def sigmoid(x):
    return 1.0 / (1.0 + jnp.exp(-x))


def local_kernel(halo, xs, maps, taps_x, taps_m, steps, rates, pack, xc, bc, cols, rows, ext):
    ext[0:8, :] = halo[...].astype(F32)
    ext[8 : 8 + TOK, 0:CH] = xs[...].astype(F32)
    ext[8 : 8 + TOK, CH : CH + 256] = maps[...].astype(F32)
    weights_x = taps_x[...].astype(F32)
    weights_m = taps_m[...].astype(F32)

    def conv(lo, width, w):
        total = w[0:1] * ext[5 : 5 + TOK, lo : lo + width]
        for k in range(1, 4):
            total = total + w[k : k + 1] * ext[5 + k : 5 + k + TOK, lo : lo + width]
        return (total * sigmoid(total)).astype(BF16)

    bc[...] = conv(CH, 256, weights_m)
    dt = jax.nn.softplus(steps[...])
    eye = lax.broadcasted_iota(jnp.int32, (HEADS, HEADS), 0) == lax.broadcasted_iota(
        jnp.int32, (HEADS, HEADS), 1
    )
    rate_row = -jnp.exp(rates[...])
    rate = jnp.sum(
        jnp.where(eye, jnp.broadcast_to(rate_row, (HEADS, HEADS)), 0.0), axis=1, keepdims=True
    )
    cum = dt * rate
    token = lax.broadcasted_iota(jnp.int32, (HEADS, TOK), 1)
    for s in (1, 2, 4, 8, 16, 32, 64, 128):
        cum = cum + jnp.where(token >= s, pltpu.roll(cum, s, 1), 0.0)
    total = cum[:, TOK - 1 : TOK]
    tail = jnp.exp(total - cum) * dt
    rows[0:HEADS, :] = cum
    rows[HEADS : 2 * HEADS, :] = dt
    stacked = jnp.concatenate(
        [tail, cum, jnp.exp(cum), jnp.zeros((128 - 3 * HEADS, TOK), F32)], axis=0
    )
    columns = jnp.transpose(stacked)
    cols[...] = columns
    lane = lax.broadcasted_iota(jnp.int32, (TOK, 128), 1)
    b = bc[:, 0:NS]
    for j in range(8):
        lo = 128 * j
        x = conv(lo, 128, weights_x[:, lo : lo + 128])
        xc[:, lo : lo + 128] = x
        tail_pair = lane_pair(lane, columns[:, 2 * j : 2 * j + 1], columns[:, 2 * j + 1 : 2 * j + 2])
        weighted = (tail_pair * x.astype(F32)).astype(BF16)
        state = lax.dot_general(
            weighted, b, (((0,), (0,)), ((), ())), preferred_element_type=F32
        )
        pack[4 * j : 4 * j + 4, 0:PART, :] = state.astype(BF16).reshape(4, PART, NS)
    row = lax.broadcasted_iota(jnp.int32, (PACK - PART, NS), 0)
    hi = total.astype(BF16).astype(F32)
    mid = (total - hi).astype(BF16).astype(F32)
    low = total - hi - mid
    for h in range(HEADS):
        piece = jnp.where(
            row == 0,
            hi[h : h + 1, :],
            jnp.where(row == 1, mid[h : h + 1, :], jnp.where(row == 2, low[h : h + 1, :], 0.0)),
        ).astype(BF16)
        pack[2 * h, PART:PACK, :] = piece
        pack[2 * h + 1, PART:PACK, :] = piece


def local_part(halo, xs, maps, taps_x, taps_m, steps, rates):
    return pl.pallas_call(
        local_kernel,
        out_shape=(
            jax.ShapeDtypeStruct((32, PACK, NS), BF16),
            jax.ShapeDtypeStruct((TOK, CH), BF16),
            jax.ShapeDtypeStruct((TOK, 256), BF16),
            jax.ShapeDtypeStruct((TOK, 128), F32),
            jax.ShapeDtypeStruct((2 * HEADS, TOK), F32),
        ),
        scratch_shapes=[pltpu.VMEM((TOK + 8, CH + 256), F32)],
        compiler_params=PARAMS,
        name="mixer_local",
    )(*[in_hbm(a) for a in (halo, xs, maps, taps_x, taps_m, steps, rates)])


def scan_kernel(got, out):
    entering = jnp.zeros((PART, NS), F32)
    for b in range(NY * NZ):
        out[b] = entering.astype(BF16)
        block = got[b].astype(F32)
        log_decay = block[PART : PART + 1] + block[PART + 1 : PART + 2] + block[PART + 2 : PART + 3]
        entering = jnp.exp(log_decay) * entering + block[0:PART]


def scan_part(got):
    return pl.pallas_call(
        scan_kernel, out_shape=jax.ShapeDtypeStruct((32, PART, NS), BF16), compiler_params=PARAMS, name="mixer_scan"
    )(got)


def inner_kernel(skip, xc, bc, cols, rows, out):
    g = dot_tt(bc[:, NS : 2 * NS], bc[:, 0:NS])
    t = lax.broadcasted_iota(jnp.int32, (TOK, TOK), 0)
    s = lax.broadcasted_iota(jnp.int32, (TOK, TOK), 1)
    g = jnp.where(t >= s, g, 0.0)
    lane = lax.broadcasted_iota(jnp.int32, (TOK, 128), 1)
    for j in range(8):
        x = xc[:, 128 * j : 128 * j + 128]
        parts = []
        for h in (2 * j, 2 * j + 1):
            gap = cols[:, HEADS + h : HEADS + h + 1] - rows[h : h + 1, :]
            mix = g * jnp.exp(jnp.minimum(gap, 0.0)) * rows[HEADS + h : HEADS + h + 1, :]
            parts.append(jnp.dot(mix.astype(BF16), x, preferred_element_type=F32))
        gain = lane_pair(lane, skip[2 * j], skip[2 * j + 1])
        out[:, 128 * j : 128 * j + 128] = lane_pair(lane, parts[0], parts[1]) + gain * x.astype(F32)


def inner_part(skip, xc, bc, cols, rows):
    vm = pl.BlockSpec(memory_space=pltpu.VMEM)
    return pl.pallas_call(
        inner_kernel,
        out_shape=jax.ShapeDtypeStruct((TOK, CH), F32),
        in_specs=[pl.BlockSpec(memory_space=pltpu.SMEM), vm, vm, vm, vm],
        compiler_params=PARAMS,
        name="mixer_inner",
    )(skip, xc, bc, cols, rows)


def project_kernel(place, y0, bc, entering, cols, gates, gain, weight, keep, send, u_ref, normed, wbuf, sems):
    block = wbuf.shape[2]
    copies = [
        pltpu.make_async_copy(weight.at[:, pl.ds(block * i, block)], wbuf.at[i], sems.at[i])
        for i in range(wbuf.shape[0])
    ]
    for copy in copies:
        copy.start()
    lane = lax.broadcasted_iota(jnp.int32, (TOK, 128), 1)
    c = bc[:, NS : 2 * NS]
    square = jnp.zeros((TOK, 128), F32)
    for j in range(8):
        lo = 128 * j
        carried = dot_tt(c, entering[lo : lo + 128, :])
        h = 2 * HEADS + 2 * j
        decay = lane_pair(lane, cols[:, h : h + 1], cols[:, h + 1 : h + 2])
        y = y0[:, lo : lo + 128] + decay * carried
        z = gates[:, lo : lo + 128].astype(F32)
        u = y * (z * sigmoid(z))
        u_ref[:, lo : lo + 128] = u
        square = square + u * u
    mean = jnp.sum(square, axis=1, keepdims=True) * (1.0 / CH)
    scale = lax.rsqrt(mean + 1e-05)
    core = place[0]
    for d in range(NX * NC):
        first = 32 * (d // NC) + 128 * jnp.where(core == d % NC, 0, 1)
        first = pl.multiple_of(first, 32)
        value = u_ref[32 * d : 32 * d + 32, :] * scale[32 * d : 32 * d + 32] * gain[...]
        normed[pl.ds(first, 32), :] = value.astype(BF16)
    rows = normed[...]
    for i, copy in enumerate(copies):
        copy.wait()
        product = jnp.dot(rows, wbuf[i], preferred_element_type=F32).astype(BF16)
        keep[:, block * i : block * i + block] = product[0:128]
        send[:, block * i : block * i + block] = product[128:256]


def project_part(place, y0, bc, entering, cols, gates, gain, weight):
    block = 1024
    vm = pl.BlockSpec(memory_space=pltpu.VMEM)
    half = jax.ShapeDtypeStruct((128, DOUT), BF16)
    return pl.pallas_call(
        project_kernel,
        out_shape=(half, half),
        in_specs=[pl.BlockSpec(memory_space=pltpu.SMEM)] + [vm] * 6 + [pl.BlockSpec(memory_space=pl.ANY)],
        scratch_shapes=[
            pltpu.VMEM((TOK, CH), F32),
            pltpu.VMEM((TOK, CH), BF16),
            pltpu.VMEM((DOUT // block, CH, block), BF16),
            pltpu.SemaphoreType.DMA((DOUT // block,)),
        ],
        compiler_params=PARAMS,
        name="mixer_project",
    )(place, y0, bc, entering, cols, gates, gain, in_hbm(weight))


def pair_sum_kernel(place, keep, got, *outs):
    x = place[1]
    for s in range(NX):
        first = pl.multiple_of(((x + s) % NX) * 32, 32)
        total = keep[pl.ds(first, 32), :].astype(F32) + got[pl.ds(first, 32), :].astype(F32)
        outs[s][...] = total.astype(BF16)


def pair_sum(place, keep, got):
    vm = pl.BlockSpec(memory_space=pltpu.VMEM)
    return pl.pallas_call(
        pair_sum_kernel,
        out_shape=(jax.ShapeDtypeStruct((32, DOUT), BF16),) * NX,
        in_specs=[pl.BlockSpec(memory_space=pltpu.SMEM), vm, vm],
        compiler_params=PARAMS,
        name="pair_sum",
    )(place, keep, got)


def prep_kernel(xs, maps, k, v, edge, kv):
    edge[:, 0:CH] = xs[...]
    edge[:, CH : CH + 256] = maps[...]
    kv[0:TOK, :] = k[...]
    for i in range(2):
        turned = jnp.transpose(v[128 * i : 128 * i + 128, :].astype(F32))
        kv[TOK + 128 * i : TOK + 128 * i + 128, :] = turned.astype(BF16)


def prep(xs, maps, k, v):
    last = lambda width: pl.BlockSpec((8, width), lambda i: (TOK // 8 - 1, 0))
    full = lambda rows, width: pl.BlockSpec((rows, width), lambda i: (0, 0))
    return pl.pallas_call(
        prep_kernel,
        grid=(1,),
        out_shape=(
            jax.ShapeDtypeStruct((8, CH + 256), BF16),
            jax.ShapeDtypeStruct((2 * TOK, HD), BF16),
        ),
        in_specs=[last(CH), last(256), full(TOK, HD), full(TOK, HD)],
        out_specs=[full(8, CH + 256), full(2 * TOK, HD)],
        compiler_params=PARAMS,
        name="prep",
    )(in_hbm(xs), in_hbm(maps), in_hbm(k), in_hbm(v))


def stack_kernel(*refs):
    for i in range(NZ):
        refs[NZ + i // 4][i % 4] = refs[i][...]


def stack(pieces):
    part = pl.BlockSpec((256, HD), lambda i: (i, 0))
    return pl.pallas_call(
        stack_kernel,
        grid=(2,),
        out_shape=(jax.ShapeDtypeStruct((NZ // 2, 2 * TOK, HD), BF16),) * 2,
        in_specs=[part] * NZ,
        out_specs=[pl.BlockSpec((NZ // 2, 256, HD), lambda i: (0, i, 0))] * 2,
        compiler_params=PARAMS,
        name="stack_row",
    )(*[in_hbm(a) for a in pieces])


GH = 4
AHEAD = 3
ACC = HD + 8
VM = pl.BlockSpec(memory_space=pltpu.VMEM)
SM = pl.BlockSpec(memory_space=pltpu.SMEM)


def in_hbm(x):
    return pltpu.with_memory_space_constraint(x, pltpu.HBM)


def in_vmem(x):
    return pltpu.with_memory_space_constraint(x, pltpu.VMEM)


def attend(queries, chunks, peaks, accs):
    heads = [(q.astype(F32) * (HD**-0.5 * LOG2E)).astype(BF16) for q in queries]
    steps = [(chunk, g) for chunk in chunks for g in range(GH)]

    def scores(step):
        (pieces, mask), g = step
        k = [p[0:TOK, :] for p in pieces]
        s = dot_tt(k[0] if len(k) == 1 else jnp.concatenate(k, axis=0), heads[g])
        return s if mask is None else mask(s)

    waiting = [scores(step) for step in steps[:AHEAD]]
    for i, ((pieces, _), g) in enumerate(steps):
        if i + AHEAD < len(steps):
            waiting.append(scores(steps[i + AHEAD]))
        s = waiting.pop(0)
        n = s.shape[0]
        best = jnp.max(s.reshape(n // 8, 8, TOK), axis=0)
        best = jnp.broadcast_to(jnp.max(best, axis=0, keepdims=True), (8, TOK))
        peak = jnp.maximum(peaks[g], best)
        weights = jnp.exp2(s - peak[0:1]).astype(BF16)
        old = accs[g] * jnp.exp2(peaks[g] - peak)[0:1]
        peaks[g] = peak
        turned = []
        for p in pieces:
            turned += [p[TOK : TOK + 128, :], p[TOK + 128 : TOK + 256, :]]
        turned = jnp.concatenate([jnp.concatenate(turned, axis=1), jnp.ones((8, n), BF16)], axis=0)
        accs[g] = old + jnp.dot(turned, weights, preferred_element_type=F32)


def head_lanes(group, g):
    return pl.ds(pl.multiple_of(GH * HD * group + HD * g, HD), HD)


def attend_group(group, q, chunks, state):
    peak, acc = state
    queries = [q[:, head_lanes(group, g)] for g in range(GH)]
    peaks = [peak[GH * group + g] for g in range(GH)]
    accs = [acc[GH * group + g] for g in range(GH)]
    attend(queries, chunks, peaks, accs)
    for g in range(GH):
        peak[GH * group + g] = peaks[g]
        acc[GH * group + g] = accs[g]


STATE = (pltpu.VMEM((QH, 8, TOK), F32), pltpu.VMEM((QH, ACC, TOK), F32))


def own_row_kernel(place, q, *refs):
    pieces, state = refs[:NZ], refs[NZ:]
    z = place[2]

    def diagonal(s):
        key = lax.broadcasted_iota(jnp.int32, (TOK, TOK), 0)
        query = lax.broadcasted_iota(jnp.int32, (TOK, TOK), 1)
        return jnp.where(key <= query, s, -1e30)

    def before(offs):
        def mask(s):
            parts = [jnp.where(o <= z, s[TOK * i : TOK * i + TOK], -1e30) for i, o in enumerate(offs)]
            return parts[0] if len(parts) == 1 else jnp.concatenate(parts, axis=0)

        return mask

    state[0][...] = jnp.full((QH, 8, TOK), -1e30, F32)
    state[1][...] = jnp.zeros((QH, ACC, TOK), F32)
    chunks = [([pieces[0]], diagonal)]
    for o in range(1, NZ, 2):
        offs = range(o, min(o + 2, NZ))
        chunks.append(([pieces[i] for i in offs], before(offs)))

    @pl.loop(0, QH // GH)
    def _(group):
        attend_group(group, q, chunks, state)


def own_row(place, q, pieces):
    return pl.pallas_call(
        own_row_kernel,
        out_shape=STATE,
        in_specs=[SM] + [VM] * (1 + NZ),
        out_specs=[VM, VM],
        compiler_params=PARAMS,
        name="attend_row",
    )(place, q, *[in_hbm(a) for a in pieces])


def rows_kernel(least, final, place, q, *refs):
    n = len(least)
    sets, outs = refs[:n], refs[n + 2 :]
    state = outs[-2:]
    y = place[3]

    for low in sorted(set(least)):

        @pl.when(y >= low)
        def _(low=low):
            pieces = [ref.at[o] for ref, at in zip(sets, least) if at == low for o in range(ref.shape[0])]
            chunks = [(pieces[o : o + 2], None) for o in range(0, len(pieces), 2)]

            @pl.loop(0, QH // GH)
            def _(group):
                attend_group(group, q, chunks, state)

    if final:
        for h in range(QH):
            value = state[1][h, 0:HD, :] / state[1][h, HD : HD + 1, :]
            outs[0][:, HD * h : HD * h + HD] = jnp.transpose(value).astype(BF16)


def other_rows(place, q, sets, least, state, final=False):
    first = 2 + len(sets)
    head = (jax.ShapeDtypeStruct((TOK, QH * HD), BF16),) if final else ()
    return pl.pallas_call(
        functools.partial(rows_kernel, least, final),
        out_shape=head + STATE,
        in_specs=[SM] + [VM] * (3 + len(sets)),
        out_specs=[VM] * (len(head) + 2),
        input_output_aliases={first: len(head), first + 1: len(head) + 1},
        compiler_params=PARAMS,
        name="attend_final" if final else "attend_rows",
    )(place, q, *[in_hbm(a) for a in sets], *[in_vmem(a) for a in state])


def along_z(step):
    return [(y * NZ + z, y * NZ + (z + step) % NZ) for y in range(NY) for z in range(NZ)]


def along_y(pairs):
    return [(a * NZ + z, b * NZ + z) for a, b in pairs for z in range(NZ)]


def along_x(step):
    return [(x * NC + c, ((x + step) % NX) * NC + c) for x in range(NX) for c in range(NC)]


def per_device(
    ssm_inputs,
    state_maps,
    ssm_gates,
    time_steps,
    log_rates,
    skip_gain,
    conv_inputs,
    conv_maps,
    norm_gain,
    out_weight,
    queries,
    attention_keys,
    values,
):
    ctx = lax.axis_index("ctx")
    tp = lax.axis_index("tp")
    place = jnp.stack([tp % NC, tp // NC, ctx % NZ, ctx // NZ]).astype(jnp.int32)
    maps = state_maps.reshape(TOK, 256)
    taps_m = conv_maps.reshape(4, 256)

    edge, kv = prep(ssm_inputs, maps, attention_keys, values)
    halo = lax.ppermute(edge, "ctx", [(i, i + 1) for i in range(NY * NZ - 1)])
    f1 = lax.ppermute(kv, "ctx", along_z(1))
    b1 = lax.ppermute(kv, "ctx", along_z(-1))
    pack, xc, bc, cols, rows = local_part(
        halo, ssm_inputs, maps, conv_inputs, taps_m, time_steps, log_rates.reshape(1, HEADS)
    )
    f2 = lax.ppermute(f1, "ctx", along_z(1))
    b2 = lax.ppermute(b1, "ctx", along_z(-1))
    got = lax.all_to_all(pack, "ctx", 0, 0)
    f3 = lax.ppermute(f2, "ctx", along_z(1))
    b3 = lax.ppermute(b2, "ctx", along_z(-1))
    y0 = inner_part(skip_gain, xc, bc, cols, rows)
    f4 = lax.ppermute(f3, "ctx", along_z(1))
    scanned = scan_part(got)
    entering = lax.all_to_all(scanned, "ctx", 0, 0).reshape(CH, NS)

    pieces = [kv, f1, f2, f3, f4, b3, b2, b1]
    near, far = stack(pieces)
    up, down = along_y([(0, 1), (1, 2), (2, 3)]), along_y([(0, 3), (1, 0)])
    yfa = lax.ppermute(near, "ctx", up)
    yba = lax.ppermute(far, "ctx", down)
    state = own_row(place, queries, pieces)
    y2f = lax.ppermute(yfa, "ctx", along_y([(1, 2), (2, 3)]))
    y2b = lax.ppermute(yba, "ctx", along_y([(3, 2), (0, 3)]))
    yfb = lax.ppermute(far, "ctx", up)
    ybb = lax.ppermute(near, "ctx", along_y([(0, 3)]))
    state = other_rows(place, queries, [yfa, yba], [1, 3], state)
    keep, send = project_part(
        place, y0, bc, entering, cols, ssm_gates, norm_gain.reshape(1, CH), out_weight
    )
    swapped = lax.ppermute(send, "tp", [(i, i ^ 1) for i in range(NX * NC)])
    state = other_rows(place, queries, [yfb, ybb], [1, 3], state)
    sums = pair_sum(place, keep, swapped)
    others = []
    for s in range(1, NX):
        others.append(lax.ppermute(sums[s], "tp", along_x(s)))
    attn_out, *_ = other_rows(place, queries, [y2f, y2b], [2, 2], state, final=True)
    total = sums[0].astype(F32)
    for a in others:
        total = total + a.astype(F32)
    ssm_out = total.astype(BF16)
    return ssm_out, attn_out


def solution(mesh):
    placed = (
        P("ctx", "tp"),
        P("ctx", "tp", None),
        P("ctx", "tp"),
        P("tp", "ctx"),
        P("tp"),
        P("tp"),
        P(None, "tp"),
        P(None, "tp", None),
        P("tp"),
        P("tp", None),
        P("ctx", "tp"),
        P("ctx", "tp"),
        P("ctx", "tp"),
    )

    return jax.shard_map(
        per_device,
        mesh=mesh,
        in_specs=placed,
        out_specs=(P(("ctx", "tp"), None), P("ctx", "tp")),
        check_vma=False,
    )
```

time: 186 us -> 141 us (0.76)
  the two profiles are of different devices: /device:TPU:248 before, /device:TPU:24 now
where the time goes in v2:
time: 141 us; the launch traced here: 140 us
  Pallas kernels  42.8 us (30%)
  starting transfers between devices  37.7 us (27%)
  waiting for transfers between devices  35.4 us (25%)
  blocking collectives  20.1 us (14%)
  local copies, waits for them, and re-layouts  2.3 us (2%)
    pallas_call x3, Pallas kernels, other_rows(): pl.pallas_call(functools.partial(rows_kernel, least, final), out_shape=he...  21.2 us
    all_to_all x1, blocking collectives, per_device(): got = lax.all_to_all(pack, 'ctx', 0, 0)  20.1 us
    ppermute x1, waiting for transfers between devices, per_device(): yfa = lax.ppermute(near, 'ctx', up)  11.5 us
    all_to_all x1, starting transfers between devices, per_device(): entering = lax.all_to_all(scanned, 'ctx', 0, 0).reshape(CH, NS)  6.96 us
    ppermute x3, starting transfers between devices, per_device(): others.append(lax.ppermute(sums[s], 'tp', along_x(s)))  6.83 us
    pallas_call x1, Pallas kernels, own_row(): pl.pallas_call(own_row_kernel, out_shape=STATE, in_specs=[SM] + [VM] * (1...  6.31 us
    ppermute x1, waiting for transfers between devices, per_device(): f1 = lax.ppermute(kv, 'ctx', along_z(1))  6.15 us
    ppermute x1, waiting for transfers between devices, per_device(): halo = lax.ppermute(edge, 'ctx', [(i, i + 1) for i in range(NY * NZ - 1)])  5.87 us
  transfers between devices with their start and end apart: 19, of which 8 were waited for; matrix products, arithmetic and copies ran while one was open for 0% of the time, Pallas kernels for 27%

profile of v2, /device:TPU:24, one launch (start us, length us, event | category | flops | bytes accessed | tf_op | source)
XLA Modules:
  0.0 140.2 jit_solution(3298918366458794668)
XLA Ops:
  1.7 3.8 %collective-permute-start = (bf16[8,1280]{1,0:T(8,128)(2,1)S(1)}, bf16[8,1280]{1,0:T(8,128)(2,1)S(1)}, u32[]{:S(2)}, u32[]{:S(2)}) collective-permute-start(bf16[8,1280]{1,0:T(8,128)(2,1)S(1)} %get-tuple-element.24), channel_id=1, source_target_pairs={{0,8},{8,16},{16,24},{24,32},{32,40},{40,48},{48,56},{56,64},{64,7... | collective-permute-start | bytes 61448 | tf_op jit(solution)/shard_map/ppermute | solution.py:452
  5.5 5.9 %collective-permute-done.halo = bf16[8,1280]{1,0:T(8,128)(2,1)S(1)} collective-permute-done((bf16[8,1280]{1,0:T(8,128)(2,1)S(1)}, bf16[8,1280]{1,0:T(8,128)(2,1)S(1)}, u32[]{:S(2)}, u32[]{:S(2)}) %collective-permute-start) | collective-permute-done | bytes 20512 | tf_op jit(solution)/shard_map/ppermute | solution.py:452
  12.0 3.7 %mixer_local.1 = (bf16[32,48,128]{2,1,0:T(8,128)(2,1)S(1)}, bf16[256,1024]{1,0:T(8,128)(2,1)S(1)}, bf16[256,256]{1,0:T(8,128)(2,1)S(1)}, f32[256,128]{1,0:T(8,128)S(1)}, f32[32,256]{1,0:T(8,128)S(1)}) custom-call(bf16[8,1280]{1,0:T(8,128)(2,1)} %copy-done.18, bf16[256,1024]{1,0:T(8,128)(2,1)} %xs.3, bf16[256,256]{1,0:T(8,128)(2,1)} %bitcast.12, ...), custom_call_target="tpu_custom_call" | custom-call | tf_op jit(solution)/shard_map/mixer_local/pallas_call | solution.py:103
  15.6 20.1 %all_to_all.10.got = bf16[32,48,128]{2,1,0:T(8,128)(2,1)S(1)} all-to-all(bf16[32,48,128]{2,1,0:T(8,128)(2,1)S(1)} %get-tuple-element.29), channel_id=1, replica_groups=mesh['ctx'=32,'tp'=8] {'ctx'}, dimensions={0} | all-to-all | bytes 786432 | tf_op jit(solution)/shard_map/all_to_all | solution.py:460
  36.5 7.0 %all-to-all-start.1 = ((bf16[32,32,128]{2,1,0:T(8,128)(2,1)}), bf16[32,32,128]{2,1,0:T(8,128)(2,1)S(1)}, u32[]{:S(2)}, u32[]{:S(2)}) async-start(bf16[32,32,128]{2,1,0:T(8,128)(2,1)} %mixer_scan.1), calls=%async_computation.1 | async-start | bytes 524288 | tf_op jit(solution)/shard_map/all_to_all | solution.py:466
  43.5 1.5 %collective-permute-start.5 = (bf16[512,128]{1,0:T(8,128)(2,1)S(1)}, bf16[512,128]{1,0:T(8,128)(2,1)S(1)}, u32[]{:S(2)}, u32[]{:S(2)}) collective-permute-start(bf16[512,128]{1,0:T(8,128)(2,1)S(1)} %get-tuple-element.36.refs_0_), channel_id=1, source_target_pairs={{0,8},{8,16},{16,24},{24,32},{32,40},{40,48},{48,56},{56,0},{64,72... | collective-permute-start | bytes 393224 | tf_op jit(solution)/shard_map/ppermute | solution.py:453
  45.0 1.8 %collective-permute-start.9 = (bf16[512,128]{1,0:T(8,128)(2,1)S(1)}, bf16[512,128]{1,0:T(8,128)(2,1)S(1)}, u32[]{:S(2)}, u32[]{:S(2)}) collective-permute-start(bf16[512,128]{1,0:T(8,128)(2,1)S(1)} %get-tuple-element.36.refs_0_), channel_id=1, source_target_pairs={{0,56},{8,0},{16,8},{24,16},{32,24},{40,32},{48,40},{56,48},{64,12... | collective-permute-start | bytes 393224 | tf_op jit(solution)/shard_map/ppermute | solution.py:454
  46.8 6.1 %collective-permute-done.5.refs_1_ = bf16[512,128]{1,0:T(8,128)(2,1)S(1)} collective-permute-done((bf16[512,128]{1,0:T(8,128)(2,1)S(1)}, bf16[512,128]{1,0:T(8,128)(2,1)S(1)}, u32[]{:S(2)}, u32[]{:S(2)}) %collective-permute-start.5) | collective-permute-done | bytes 131104 | tf_op jit(solution)/shard_map/ppermute | solution.py:453
  53.0 1.9 %mixer_inner.1.y0 = f32[256,1024]{1,0:T(8,128)S(1)} custom-call(f32[16]{0:T(128)S(1)} %copy-done.4, bf16[256,1024]{1,0:T(8,128)(2,1)S(1)} %get-tuple-element.25.xc, bf16[256,256]{1,0:T(8,128)(2,1)S(1)} %get-tuple-element.26.bc, f32[256,128]{1,0:T(8,128)S(1)} %get-tuple-element.27.cols, f32[32,256]{1,0:T(8,128)S(1)} %get-tuple-element.28.rows), custom_call_target="tpu_custom_call" | custom-call | tf_op jit(solution)/shard_map/mixer_inner/pallas_call | solution.py:152
  55.0 3.3 %collective-permute-start.10 = (bf16[512,128]{1,0:T(8,128)(2,1)S(1)}, bf16[512,128]{1,0:T(8,128)(2,1)S(1)}, u32[]{:S(2)}, u32[]{:S(2)}) collective-permute-start(bf16[512,128]{1,0:T(8,128)(2,1)S(1)} %collective-permute-done.9.refs_7_), channel_id=1, source_target_pairs={{0,56},{8,0},{16,8},{24,16},{32,24},{40,32},{48,40},{56,48},{64,12... | collective-permute-start | bytes 393224 | tf_op jit(solution)/shard_map/ppermute | solution.py:459
  59.4 5.8 %mixer_project.1 = (bf16[128,4096]{1,0:T(8,128)(2,1)S(1)}, bf16[128,4096]{1,0:T(8,128)(2,1)S(1)}) custom-call(s32[4]{0:T(128)S(1)} %pad_add_fusion.place, f32[256,1024]{1,0:T(8,128)S(1)} %mixer_inner.1.y0, bf16[256,256]{1,0:T(8,128)(2,1)S(1)} %get-tuple-element.26.bc, bf16[1024,128]{1,0:T(8,128)(2,1)S(1)} %bitcast.9, f32[256,128]{1,0:T(8,128)S(1)} %get-tuple-element.27.cols, ...), custom_call_target="tpu_custom_call" | custom-call | tf_op jit(solution)/shard_map/mixer_project/pallas_call | solution.py:202
  65.4 3.5 %collective-permute-start.11 = (bf16[512,128]{1,0:T(8,128)(2,1)S(1)}, bf16[512,128]{1,0:T(8,128)(2,1)S(1)}, u32[]{:S(2)}, u32[]{:S(2)}) collective-permute-start(bf16[512,128]{1,0:T(8,128)(2,1)S(1)} %collective-permute-done.10.refs_6_), channel_id=1, source_target_pairs={{0,56},{8,0},{16,8},{24,16},{32,24},{40,32},{48,40},{56,48},{64,12... | collective-permute-start | bytes 393224 | tf_op jit(solution)/shard_map/ppermute | solution.py:462
  68.8 3.1 %collective-permute-done.11.refs_5_ = bf16[512,128]{1,0:T(8,128)(2,1)S(1)} collective-permute-done((bf16[512,128]{1,0:T(8,128)(2,1)S(1)}, bf16[512,128]{1,0:T(8,128)(2,1)S(1)}, u32[]{:S(2)}, u32[]{:S(2)}) %collective-permute-start.11) | collective-permute-done | bytes 131104 | tf_op jit(solution)/shard_map/ppermute | solution.py:462
  72.0 3.4 %collective-permute-done.8.refs_4_ = bf16[512,128]{1,0:T(8,128)(2,1)S(1)} collective-permute-done((bf16[512,128]{1,0:T(8,128)(2,1)S(1)}, bf16[512,128]{1,0:T(8,128)(2,1)S(1)}, u32[]{:S(2)}, u32[]{:S(2)}) %collective-permute-start.8) | collective-permute-done | bytes 131104 | tf_op jit(solution)/shard_map/ppermute | solution.py:464
  82.8 11.5 %collective-permute-done.12.refs_0_ = bf16[4,512,128]{2,1,0:T(8,128)(2,1)S(1)} collective-permute-done((bf16[4,512,128]{2,1,0:T(8,128)(2,1)S(1)}, bf16[4,512,128]{2,1,0:T(8,128)(2,1)S(1)}, u32[]{:S(2)}, u32[]{:S(2)}) %collective-permute-start.12) | collective-permute-done | bytes 524320 | tf_op jit(solution)/shard_map/ppermute | solution.py:471
  96.8 3.3 %collective-permute-start.15 = (bf16[4,512,128]{2,1,0:T(8,128)(2,1)S(1)}, bf16[4,512,128]{2,1,0:T(8,128)(2,1)S(1)}, u32[]{:S(2)}, u32[]{:S(2)}) collective-permute-start(bf16[4,512,128]{2,1,0:T(8,128)(2,1)S(1)} %collective-permute-done.14.refs_1_), channel_id=1, source_target_pairs={{192,128},{200,136},{208,144},{216,152},{224,160},{232,168},{240,1... | collective-permute-start | bytes 1572872 | tf_op jit(solution)/shard_map/ppermute | solution.py:475
  100.9 1.6 %collective-permute-start.2 = (bf16[32,4096]{1,0:T(8,128)(2,1)S(1)}, bf16[32,4096]{1,0:T(8,128)(2,1)S(1)}, u32[]{:S(2)}, u32[]{:S(2)}) collective-permute-start(bf16[32,4096]{1,0:T(8,128)(2,1)S(1)} %get-tuple-element.33), channel_id=1, source_target_pairs={{0,2},{1,3},{2,4},{3,5},{4,6},{5,7},{6,0},{7,1},{8,10},{9,11},{10,... | collective-permute-start | bytes 786440 | tf_op jit(solution)/shard_map/ppermute | solution.py:487
  102.5 3.0 %collective-permute-done.16.refs_0_ = bf16[4,512,128]{2,1,0:T(8,128)(2,1)S(1)} collective-permute-done((bf16[4,512,128]{2,1,0:T(8,128)(2,1)S(1)}, bf16[4,512,128]{2,1,0:T(8,128)(2,1)S(1)}, u32[]{:S(2)}, u32[]{:S(2)}) %collective-permute-start.16) | collective-permute-done | bytes 524320 | tf_op jit(solution)/shard_map/ppermute | solution.py:476
  105.5 3.0 %collective-permute-start.3 = (bf16[32,4096]{1,0:T(8,128)(2,1)S(1)}, bf16[32,4096]{1,0:T(8,128)(2,1)S(1)}, u32[]{:S(2)}, u32[]{:S(2)}) collective-permute-start(bf16[32,4096]{1,0:T(8,128)(2,1)S(1)} %get-tuple-element.34), channel_id=1, source_target_pairs={{0,4},{1,5},{2,6},{3,7},{4,0},{5,1},{6,2},{7,3},{8,12},{9,13},{10,... | collective-permute-start | bytes 786440 | tf_op jit(solution)/shard_map/ppermute | solution.py:487
  108.5 2.2 %collective-permute-start.4 = (bf16[32,4096]{1,0:T(8,128)(2,1)S(1)}, bf16[32,4096]{1,0:T(8,128)(2,1)S(1)}, u32[]{:S(2)}, u32[]{:S(2)}) collective-permute-start(bf16[32,4096]{1,0:T(8,128)(2,1)S(1)} %get-tuple-element.35), channel_id=1, source_target_pairs={{0,6},{1,7},{2,0},{3,1},{4,2},{5,3},{6,4},{7,5},{8,14},{9,15},{10,... | collective-permute-start | bytes 786440 | tf_op jit(solution)/shard_map/ppermute | solution.py:487
  110.8 6.3 %attend_row.1 = (f32[8,8,256]{2,1,0:T(8,128)S(1)}, f32[8,136,256]{2,1,0:T(8,128)S(1)}) custom-call(s32[4]{0:T(128)S(1)} %pad_add_fusion.place, bf16[256,1024]{1,0:T(8,128)(2,1)S(1)} %copy-done, bf16[512,128]{1,0:T(8,128)(2,1)} %copy-done.2, bf16[512,128]{1,0:T(8,128)(2,1)} %copy-done.11, bf16[512,128]{1,0:T(8,128)(2,1)} %copy-done.13, ...), custom_call_target="tpu_custom_call" | custom-call | tf_op jit(solution)/shard_map/attend_row/pallas_call | solution.py:371
  117.1 7.0 %attend_rows.2 = (f32[8,8,256]{2,1,0:T(8,128)S(1)}, f32[8,136,256]{2,1,0:T(8,128)S(1)}) custom-call(s32[4]{0:T(128)S(1)} %pad_add_fusion.place, bf16[256,1024]{1,0:T(8,128)(2,1)S(1)} %copy-done, bf16[4,512,128]{2,1,0:T(8,128)(2,1)} %copy-done.5, bf16[4,512,128]{2,1,0:T(8,128)(2,1)} %copy-done.6, ...), custom_call_target="tpu_custom_call", output_to_operand_aliasing={{0}: (4, {}), {1}: (5, {})} | custom-call | tf_op jit(solution)/shard_map/attend_rows/pallas_call | solution.py:407
  124.1 7.2 %attend_rows.3 = (f32[8,8,256]{2,1,0:T(8,128)S(1)}, f32[8,136,256]{2,1,0:T(8,128)S(1)}) custom-call(s32[4]{0:T(128)S(1)} %pad_add_fusion.place, bf16[256,1024]{1,0:T(8,128)(2,1)S(1)} %copy-done, bf16[4,512,128]{2,1,0:T(8,128)(2,1)} %copy-done.9, bf16[4,512,128]{2,1,0:T(8,128)(2,1)} %copy-done.10, ...), custom_call_target="tpu_custom_call", output_to_operand_aliasing={{0}: (4, {}), {1}: (5, {})} | custom-call | tf_op jit(solution)/shard_map/attend_rows/pallas_call | solution.py:407
  132.3 7.1 %attend_final.1 = (bf16[256,1024]{1,0:T(8,128)(2,1)}, f32[8,8,256]{2,1,0:T(8,128)S(1)}, f32[8,136,256]{2,1,0:T(8,128)S(1)}) custom-call(s32[4]{0:T(128)S(1)} %pad_add_fusion.place, bf16[256,1024]{1,0:T(8,128)(2,1)S(1)} %copy-done, bf16[4,512,128]{2,1,0:T(8,128)(2,1)} %copy-done.7, ...), custom_call_target="tpu_custom_call", output_to_operand_aliasing={{1}: (4, {}), {2}: (5, {})} | custom-call | tf_op jit(solution)/shard_map/attend_final/pallas_call | solution.py:407
  (66 shorter events, 16.2 us)
Async XLA Ops:
  1.6 43.4 %copy-start.2 = (bf16[512,128]{1,0:T(8,128)(2,1)}, bf16[512,128]{1,0:T(8,128)(2,1)S(1)}, u32[]{:S(2)}) copy-start(bf16[512,128]{1,0:T(8,128)(2,1)S(1)} %get-tuple-element.36.refs_0_) | copy-start | bytes 393220
  1.7 9.7 %collective-permute-start = (bf16[8,1280]{1,0:T(8,128)(2,1)S(1)}, bf16[8,1280]{1,0:T(8,128)(2,1)S(1)}, u32[]{:S(2)}, u32[]{:S(2)}) collective-permute-start(bf16[8,1280]{1,0:T(8,128)(2,1)S(1)} %get-tuple-element.24), channel_id=1, source_target_pairs={{0,8},{8,16},{16,24},{24,32},{32,40},{40,48},{48,56},{56,64},{64,7... | collective-permute-start | bytes 61448 | tf_op jit(solution)/shard_map/ppermute | solution.py:452
  15.6 37.4 %copy-start.4 = (f32[16]{0:T(128)S(1)}, f32[16]{0:T(128)}, u32[]{:S(2)}) copy-start(f32[16]{0:T(128)} %skip.1) | copy-start | bytes 196
  36.5 22.9 %all-to-all-start.1 = ((bf16[32,32,128]{2,1,0:T(8,128)(2,1)}), bf16[32,32,128]{2,1,0:T(8,128)(2,1)S(1)}, u32[]{:S(2)}, u32[]{:S(2)}) async-start(bf16[32,32,128]{2,1,0:T(8,128)(2,1)} %mixer_scan.1), calls=%async_computation.1 | async-start | bytes 524288 | tf_op jit(solution)/shard_map/all_to_all | solution.py:466
  43.5 9.5 %collective-permute-start.5 = (bf16[512,128]{1,0:T(8,128)(2,1)S(1)}, bf16[512,128]{1,0:T(8,128)(2,1)S(1)}, u32[]{:S(2)}, u32[]{:S(2)}) collective-permute-start(bf16[512,128]{1,0:T(8,128)(2,1)S(1)} %get-tuple-element.36.refs_0_), channel_id=1, source_target_pairs={{0,8},{8,16},{16,24},{24,32},{32,40},{40,48},{48,56},{56,0},{64,72... | collective-permute-start | bytes 393224 | tf_op jit(solution)/shard_map/ppermute | solution.py:453
  45.0 9.9 %collective-permute-start.9 = (bf16[512,128]{1,0:T(8,128)(2,1)S(1)}, bf16[512,128]{1,0:T(8,128)(2,1)S(1)}, u32[]{:S(2)}, u32[]{:S(2)}) collective-permute-start(bf16[512,128]{1,0:T(8,128)(2,1)S(1)} %get-tuple-element.36.refs_0_), channel_id=1, source_target_pairs={{0,56},{8,0},{16,8},{24,16},{32,24},{40,32},{48,40},{56,48},{64,12... | collective-permute-start | bytes 393224 | tf_op jit(solution)/shard_map/ppermute | solution.py:454
  53.0 6.4 %collective-permute-start.6 = (bf16[512,128]{1,0:T(8,128)(2,1)S(1)}, bf16[512,128]{1,0:T(8,128)(2,1)S(1)}, u32[]{:S(2)}, u32[]{:S(2)}) collective-permute-start(bf16[512,128]{1,0:T(8,128)(2,1)S(1)} %collective-permute-done.5.refs_1_), channel_id=1, source_target_pairs={{0,8},{8,16},{16,24},{24,32},{32,40},{40,48},{48,56},{56,0},{64,72... | collective-permute-start | bytes 393224 | tf_op jit(solution)/shard_map/ppermute | solution.py:458
  55.0 10.4 %collective-permute-start.10 = (bf16[512,128]{1,0:T(8,128)(2,1)S(1)}, bf16[512,128]{1,0:T(8,128)(2,1)S(1)}, u32[]{:S(2)}, u32[]{:S(2)}) collective-permute-start(bf16[512,128]{1,0:T(8,128)(2,1)S(1)} %collective-permute-done.9.refs_7_), channel_id=1, source_target_pairs={{0,56},{8,0},{16,8},{24,16},{32,24},{40,32},{48,40},{56,48},{64,12... | collective-permute-start | bytes 393224 | tf_op jit(solution)/shard_map/ppermute | solution.py:459
  59.4 9.4 %collective-permute-start.7 = (bf16[512,128]{1,0:T(8,128)(2,1)S(1)}, bf16[512,128]{1,0:T(8,128)(2,1)S(1)}, u32[]{:S(2)}, u32[]{:S(2)}) collective-permute-start(bf16[512,128]{1,0:T(8,128)(2,1)S(1)} %collective-permute-done.6.refs_2_), channel_id=1, source_target_pairs={{0,8},{8,16},{16,24},{24,32},{32,40},{40,48},{48,56},{56,0},{64,72... | collective-permute-start | bytes 393224 | tf_op jit(solution)/shard_map/ppermute | solution.py:461
  65.2 34.9 %collective-permute-start.1 = (bf16[128,4096]{1,0:T(8,128)(2,1)S(1)}, bf16[128,4096]{1,0:T(8,128)(2,1)S(1)}, u32[]{:S(2)}, u32[]{:S(2)}) collective-permute-start(bf16[128,4096]{1,0:T(8,128)(2,1)S(1)} %get-tuple-element.31), channel_id=1, source_target_pairs={{0,1},{1,0},{2,3},{3,2},{4,5},{5,4},{6,7},{7,6},{8,9},{9,8},{10,11... | collective-permute-start | bytes 3145736 | tf_op jit(solution)/shard_map/ppermute | solution.py:482
  65.4 6.6 %collective-permute-start.11 = (bf16[512,128]{1,0:T(8,128)(2,1)S(1)}, bf16[512,128]{1,0:T(8,128)(2,1)S(1)}, u32[]{:S(2)}, u32[]{:S(2)}) collective-permute-start(bf16[512,128]{1,0:T(8,128)(2,1)S(1)} %collective-permute-done.10.refs_6_), channel_id=1, source_target_pairs={{0,56},{8,0},{16,8},{24,16},{32,24},{40,32},{48,40},{56,48},{64,12... | collective-permute-start | bytes 393224 | tf_op jit(solution)/shard_map/ppermute | solution.py:462
  68.8 6.6 %collective-permute-start.8 = (bf16[512,128]{1,0:T(8,128)(2,1)S(1)}, bf16[512,128]{1,0:T(8,128)(2,1)S(1)}, u32[]{:S(2)}, u32[]{:S(2)}) collective-permute-start(bf16[512,128]{1,0:T(8,128)(2,1)S(1)} %collective-permute-done.7.refs_3_), channel_id=1, source_target_pairs={{0,8},{8,16},{16,24},{24,32},{32,40},{40,48},{48,56},{56,0},{64,72... | collective-permute-start | bytes 393224 | tf_op jit(solution)/shard_map/ppermute | solution.py:464
  77.4 33.3 %copy-start = (bf16[256,1024]{1,0:T(8,128)(2,1)S(1)}, bf16[256,1024]{1,0:T(8,128)(2,1)}, u32[]{:S(2)}) copy-start(bf16[256,1024]{1,0:T(8,128)(2,1)} %q.7) | copy-start | bytes 1572868
  77.4 16.8 %collective-permute-start.12 = (bf16[4,512,128]{2,1,0:T(8,128)(2,1)S(1)}, bf16[4,512,128]{2,1,0:T(8,128)(2,1)S(1)}, u32[]{:S(2)}, u32[]{:S(2)}) collective-permute-start(bf16[4,512,128]{2,1,0:T(8,128)(2,1)S(1)} %get-tuple-element.37), channel_id=1, source_target_pairs={{0,64},{8,72},{16,80},{24,88},{32,96},{40,104},{48,112},{56,120},{... | collective-permute-start | bytes 1572872 | tf_op jit(solution)/shard_map/ppermute | solution.py:471
  78.9 17.9 %collective-permute-start.14 = (bf16[4,512,128]{2,1,0:T(8,128)(2,1)S(1)}, bf16[4,512,128]{2,1,0:T(8,128)(2,1)S(1)}, u32[]{:S(2)}, u32[]{:S(2)}) collective-permute-start(bf16[4,512,128]{2,1,0:T(8,128)(2,1)S(1)} %get-tuple-element.38), channel_id=1, source_target_pairs={{0,192},{8,200},{16,208},{24,216},{32,224},{40,232},{48,240},{56,2... | collective-permute-start | bytes 1572872 | tf_op jit(solution)/shard_map/ppermute | solution.py:472
  80.2 25.3 %collective-permute-start.16 = (bf16[4,512,128]{2,1,0:T(8,128)(2,1)S(1)}, bf16[4,512,128]{2,1,0:T(8,128)(2,1)S(1)}, u32[]{:S(2)}, u32[]{:S(2)}) collective-permute-start(bf16[4,512,128]{2,1,0:T(8,128)(2,1)S(1)} %get-tuple-element.38), channel_id=1, source_target_pairs={{0,64},{8,72},{16,80},{24,88},{32,96},{40,104},{48,112},{56,120},{... | collective-permute-start | bytes 1572872 | tf_op jit(solution)/shard_map/ppermute | solution.py:476
  81.5 27.1 %collective-permute-start.17 = (bf16[4,512,128]{2,1,0:T(8,128)(2,1)S(1)}, bf16[4,512,128]{2,1,0:T(8,128)(2,1)S(1)}, u32[]{:S(2)}, u32[]{:S(2)}) collective-permute-start(bf16[4,512,128]{2,1,0:T(8,128)(2,1)S(1)} %get-tuple-element.37), channel_id=1, source_target_pairs={{0,192},{8,200},{16,208},{24,216},{32,224},{40,232},{48,240},{56,2... | collective-permute-start | bytes 1572872 | tf_op jit(solution)/shard_map/ppermute | solution.py:477
  94.3 22.8 %copy-start.5 = (bf16[4,512,128]{2,1,0:T(8,128)(2,1)}, bf16[4,512,128]{2,1,0:T(8,128)(2,1)S(1)}, u32[]{:S(2)}) copy-start(bf16[4,512,128]{2,1,0:T(8,128)(2,1)S(1)} %collective-permute-done.12.refs_0_) | copy-start | bytes 1572868
  94.3 37.0 %collective-permute-start.13 = (bf16[4,512,128]{2,1,0:T(8,128)(2,1)S(1)}, bf16[4,512,128]{2,1,0:T(8,128)(2,1)S(1)}, u32[]{:S(2)}, u32[]{:S(2)}) collective-permute-start(bf16[4,512,128]{2,1,0:T(8,128)(2,1)S(1)} %collective-permute-done.12.refs_0_), channel_id=1, source_target_pairs={{64,128},{72,136},{80,144},{88,152},{96,160},{104,168},{112,176},{... | collective-permute-start | bytes 1572872 | tf_op jit(solution)/shard_map/ppermute | solution.py:474
  96.8 20.3 %copy-start.6 = (bf16[4,512,128]{2,1,0:T(8,128)(2,1)}, bf16[4,512,128]{2,1,0:T(8,128)(2,1)S(1)}, u32[]{:S(2)}) copy-start(bf16[4,512,128]{2,1,0:T(8,128)(2,1)S(1)} %collective-permute-done.14.refs_1_) | copy-start | bytes 1572868
  96.8 34.6 %collective-permute-start.15 = (bf16[4,512,128]{2,1,0:T(8,128)(2,1)S(1)}, bf16[4,512,128]{2,1,0:T(8,128)(2,1)S(1)}, u32[]{:S(2)}, u32[]{:S(2)}) collective-permute-start(bf16[4,512,128]{2,1,0:T(8,128)(2,1)S(1)} %collective-permute-done.14.refs_1_), channel_id=1, source_target_pairs={{192,128},{200,136},{208,144},{216,152},{224,160},{232,168},{240,1... | collective-permute-start | bytes 1572872 | tf_op jit(solution)/shard_map/ppermute | solution.py:475
  100.9 38.5 %collective-permute-start.2 = (bf16[32,4096]{1,0:T(8,128)(2,1)S(1)}, bf16[32,4096]{1,0:T(8,128)(2,1)S(1)}, u32[]{:S(2)}, u32[]{:S(2)}) collective-permute-start(bf16[32,4096]{1,0:T(8,128)(2,1)S(1)} %get-tuple-element.33), channel_id=1, source_target_pairs={{0,2},{1,3},{2,4},{3,5},{4,6},{5,7},{6,0},{7,1},{8,10},{9,11},{10,... | collective-permute-start | bytes 786440 | tf_op jit(solution)/shard_map/ppermute | solution.py:487
  105.5 33.9 %collective-permute-start.3 = (bf16[32,4096]{1,0:T(8,128)(2,1)S(1)}, bf16[32,4096]{1,0:T(8,128)(2,1)S(1)}, u32[]{:S(2)}, u32[]{:S(2)}) collective-permute-start(bf16[32,4096]{1,0:T(8,128)(2,1)S(1)} %get-tuple-element.34), channel_id=1, source_target_pairs={{0,4},{1,5},{2,6},{3,7},{4,0},{5,1},{6,2},{7,3},{8,12},{9,13},{10,... | collective-permute-start | bytes 786440 | tf_op jit(solution)/shard_map/ppermute | solution.py:487
  108.5 30.9 %collective-permute-start.4 = (bf16[32,4096]{1,0:T(8,128)(2,1)S(1)}, bf16[32,4096]{1,0:T(8,128)(2,1)S(1)}, u32[]{:S(2)}, u32[]{:S(2)}) collective-permute-start(bf16[32,4096]{1,0:T(8,128)(2,1)S(1)} %get-tuple-element.35), channel_id=1, source_target_pairs={{0,6},{1,7},{2,0},{3,1},{4,2},{5,3},{6,4},{7,5},{8,14},{9,15},{10,... | collective-permute-start | bytes 786440 | tf_op jit(solution)/shard_map/ppermute | solution.py:487
  (14 other events, 117.5 us)

commit v3 on v2

--- a/solution.py
+++ b/solution.py
@@ -18,7 +18,7 @@
 NY, NZ = 4, 8
 NX, NC = 4, 2
 PART = 32
-PACK = 48
+PACK = 40
 QH = 8
 HD = 128
 DOUT = 4096
@@ -277,7 +277,6 @@
     )(*[in_hbm(a) for a in pieces])
 
 
-GH = 4
 AHEAD = 3
 ACC = HD + 8
 VM = pl.BlockSpec(memory_space=pltpu.VMEM)
@@ -294,7 +293,7 @@
 
 def attend(queries, chunks, peaks, accs):
     heads = [(q.astype(F32) * (HD**-0.5 * LOG2E)).astype(BF16) for q in queries]
-    steps = [(chunk, g) for chunk in chunks for g in range(GH)]
+    steps = [(chunk, g) for chunk in chunks for g in range(len(heads))]
 
     def scores(step):
         (pieces, mask), g = step
@@ -321,26 +320,27 @@
         accs[g] = old + jnp.dot(turned, weights, preferred_element_type=F32)
 
 
-def head_lanes(group, g):
-    return pl.ds(pl.multiple_of(GH * HD * group + HD * g, HD), HD)
-
-
-def attend_group(group, q, chunks, state):
+def attend_all(together, q, chunks, state):
     peak, acc = state
-    queries = [q[:, head_lanes(group, g)] for g in range(GH)]
-    peaks = [peak[GH * group + g] for g in range(GH)]
-    accs = [acc[GH * group + g] for g in range(GH)]
-    attend(queries, chunks, peaks, accs)
-    for g in range(GH):
-        peak[GH * group + g] = peaks[g]
-        acc[GH * group + g] = accs[g]
+
+    @pl.loop(0, QH // together)
+    def _(group):
+        first = together * group
+        lanes = [pl.ds(pl.multiple_of(HD * (first + g), HD), HD) for g in range(together)]
+        peaks = [peak[first + g] for g in range(together)]
+        accs = [acc[first + g] for g in range(together)]
+        attend([q[:, at] for at in lanes], chunks, peaks, accs)
+        for g in range(together):
+            peak[first + g] = peaks[g]
+            acc[first + g] = accs[g]
 
 
 STATE = (pltpu.VMEM((QH, 8, TOK), F32), pltpu.VMEM((QH, ACC, TOK), F32))
 
 
-def own_row_kernel(place, q, *refs):
-    pieces, state = refs[:NZ], refs[NZ:]
+def own_row_kernel(offsets, place, q, *refs):
+    n = len(offsets)
+    pieces, state = refs[:n], refs[-2:]
     z = place[2]
 
     def diagonal(s):
@@ -355,27 +355,30 @@
 
         return mask
 
-    state[0][...] = jnp.full((QH, 8, TOK), -1e30, F32)
-    state[1][...] = jnp.zeros((QH, ACC, TOK), F32)
-    chunks = [([pieces[0]], diagonal)]
-    for o in range(1, NZ, 2):
-        offs = range(o, min(o + 2, NZ))
-        chunks.append(([pieces[i] for i in offs], before(offs)))
-
-    @pl.loop(0, QH // GH)
-    def _(group):
-        attend_group(group, q, chunks, state)
-
-
-def own_row(place, q, pieces):
-    return pl.pallas_call(
-        own_row_kernel,
+    chunks = []
+    at = 0
+    if offsets[0] == 0:
+        at = 1
+        chunks.append(([pieces[0]], diagonal))
+        state[0][...] = jnp.full((QH, 8, TOK), -1e30, F32)
+        state[1][...] = jnp.zeros((QH, ACC, TOK), F32)
+    for o in range(at, n, 2):
+        chunks.append((list(pieces[o : o + 2]), before(offsets[o : o + 2])))
+
+    attend_all(QH, q, chunks, state)
+
+
+def own_row(place, q, pieces, offsets, state=()):
+    first = 2 + len(pieces)
+    return pl.pallas_call(
+        functools.partial(own_row_kernel, offsets),
         out_shape=STATE,
-        in_specs=[SM] + [VM] * (1 + NZ),
+        in_specs=[SM] + [VM] * (1 + len(pieces) + len(state)),
         out_specs=[VM, VM],
+        input_output_aliases={first: 0, first + 1: 1} if state else {},
         compiler_params=PARAMS,
         name="attend_row",
-    )(place, q, *[in_hbm(a) for a in pieces])
+    )(place, q, *[in_hbm(a) for a in pieces], *[in_vmem(a) for a in state])
 
 
 def rows_kernel(least, final, place, q, *refs):
@@ -390,10 +393,7 @@
         def _(low=low):
             pieces = [ref.at[o] for ref, at in zip(sets, least) if at == low for o in range(ref.shape[0])]
             chunks = [(pieces[o : o + 2], None) for o in range(0, len(pieces), 2)]
-
-            @pl.loop(0, QH // GH)
-            def _(group):
-                attend_group(group, q, chunks, state)
+            attend_all(QH if len(pieces) < NZ else QH // 2, q, chunks, state)
 
     if final:
         for h in range(QH):
@@ -470,7 +470,7 @@
     up, down = along_y([(0, 1), (1, 2), (2, 3)]), along_y([(0, 3), (1, 0)])
     yfa = lax.ppermute(near, "ctx", up)
     yba = lax.ppermute(far, "ctx", down)
-    state = own_row(place, queries, pieces)
+    state = own_row(place, queries, pieces, tuple(range(NZ)))
     y2f = lax.ppermute(yfa, "ctx", along_y([(1, 2), (2, 3)]))
     y2b = lax.ppermute(yba, "ctx", along_y([(3, 2), (0, 3)]))
     yfb = lax.ppermute(far, "ctx", up)
@@ -480,12 +480,11 @@
         place, y0, bc, entering, cols, ssm_gates, norm_gain.reshape(1, CH), out_weight
     )
     swapped = lax.ppermute(send, "tp", [(i, i ^ 1) for i in range(NX * NC)])
-    state = other_rows(place, queries, [yfb, ybb], [1, 3], state)
     sums = pair_sum(place, keep, swapped)
     others = []
     for s in range(1, NX):
         others.append(lax.ppermute(sums[s], "tp", along_x(s)))
-    attn_out, *_ = other_rows(place, queries, [y2f, y2b], [2, 2], state, final=True)
+    attn_out, *_ = other_rows(place, queries, [yfb, ybb, y2f, y2b], [1, 3, 2, 2], state, final=True)
     total = sums[0].astype(F32)
     for a in others:
         total = total + a.astype(F32)

time: 141 us -> 137 us (0.972)
  starting transfers between devices: 37.7 us -> 34.9 us
  Pallas kernels: 42.8 us -> 40 us
  waiting for transfers between devices: 35.4 us -> 38 us
    ppermute x1, waiting for transfers between devices: 11.5 us -> 0.01 us  [per_device(): yfa = lax.ppermute(near, 'ctx', up)]
    ppermute x1, waiting for transfers between devices: 1.22 us -> 12.7 us  [per_device(): yba = lax.ppermute(far, 'ctx', down)]
    ppermute x1, waiting for transfers between devices: 2.99 us -> 5.71 us  [per_device(): yfb = lax.ppermute(far, 'ctx', up)]
    pallas_call x3 -> x2, Pallas kernels: 21.2 us -> 18.9 us  [other_rows(): pl.pallas_call(functools.partial(rows_kernel, least, final), out_shape=he...]
    ppermute x1, starting transfers between devices: 3.35 us -> 1.91 us  [per_device(): y2b = lax.ppermute(yba, 'ctx', along_y([(3, 2), (0, 3)]))]
  transfers between devices with their start and end apart: 19 -> 19, of which waited for: 8 -> 7; matrix products, arithmetic and copies ran while one was open for 0% -> 0% of each run, Pallas kernels for 27% -> 25%
where the time goes in v3:
time: 137 us; the launch traced here: 136 us
  Pallas kernels  40 us (29%)
  waiting for transfers between devices  38 us (28%)
  starting transfers between devices  34.9 us (25%)
  blocking collectives  19 us (14%)
  local copies, waits for them, and re-layouts  2.27 us (2%)
    all_to_all x1, blocking collectives, per_device(): got = lax.all_to_all(pack, 'ctx', 0, 0)  19 us
    pallas_call x2, Pallas kernels, other_rows(): pl.pallas_call(functools.partial(rows_kernel, least, final), out_shape=he...  18.9 us
    ppermute x1, waiting for transfers between devices, per_device(): yba = lax.ppermute(far, 'ctx', down)  12.7 us
    all_to_all x1, starting transfers between devices, per_device(): entering = lax.all_to_all(scanned, 'ctx', 0, 0).reshape(CH, NS)  6.65 us
    ppermute x1, waiting for transfers between devices, per_device(): f1 = lax.ppermute(kv, 'ctx', along_z(1))  5.94 us
    ppermute x1, waiting for transfers between devices, per_device(): halo = lax.ppermute(edge, 'ctx', [(i, i + 1) for i in range(NY * NZ - 1)])  5.87 us
    pallas_call x1, Pallas kernels, project_part(): pl.pallas_call(project_kernel, out_shape=(half, half), in_specs=[pl.Block...  5.77 us
    pallas_call x1, Pallas kernels, own_row(): pl.pallas_call(functools.partial(own_row_kernel, offsets), out_shape=STAT...  5.75 us
  transfers between devices with their start and end apart: 19, of which 7 were waited for; matrix products, arithmetic and copies ran while one was open for 0% of the time, Pallas kernels for 25%

profile of v3, /device:TPU:24, one launch (start us, length us, event | category | flops | bytes accessed | tf_op | source)
XLA Modules:
  0.0 136.0 jit_solution(7464029010454942478)
XLA Ops:
  1.7 3.8 %collective-permute-start = (bf16[8,1280]{1,0:T(8,128)(2,1)S(1)}, bf16[8,1280]{1,0:T(8,128)(2,1)S(1)}, u32[]{:S(2)}, u32[]{:S(2)}) collective-permute-start(bf16[8,1280]{1,0:T(8,128)(2,1)S(1)} %get-tuple-element.22), channel_id=1, source_target_pairs={{0,8},{8,16},{16,24},{24,32},{32,40},{40,48},{48,56},{56,64},{64,7... | collective-permute-start | bytes 61448 | tf_op jit(solution)/shard_map/ppermute | solution.py:452
  5.5 5.9 %collective-permute-done.halo = bf16[8,1280]{1,0:T(8,128)(2,1)S(1)} collective-permute-done((bf16[8,1280]{1,0:T(8,128)(2,1)S(1)}, bf16[8,1280]{1,0:T(8,128)(2,1)S(1)}, u32[]{:S(2)}, u32[]{:S(2)}) %collective-permute-start) | collective-permute-done | bytes 20512 | tf_op jit(solution)/shard_map/ppermute | solution.py:452
  12.0 3.7 %mixer_local.1 = (bf16[32,40,128]{2,1,0:T(8,128)(2,1)S(1)}, bf16[256,1024]{1,0:T(8,128)(2,1)S(1)}, bf16[256,256]{1,0:T(8,128)(2,1)S(1)}, f32[256,128]{1,0:T(8,128)S(1)}, f32[32,256]{1,0:T(8,128)S(1)}) custom-call(bf16[8,1280]{1,0:T(8,128)(2,1)} %copy-done.18, bf16[256,1024]{1,0:T(8,128)(2,1)} %xs.3, bf16[256,256]{1,0:T(8,128)(2,1)} %bitcast.12, ...), custom_call_target="tpu_custom_call" | custom-call | tf_op jit(solution)/shard_map/mixer_local/pallas_call | solution.py:103
  15.6 19.0 %all_to_all.10.got = bf16[32,40,128]{2,1,0:T(8,128)(2,1)S(1)} all-to-all(bf16[32,40,128]{2,1,0:T(8,128)(2,1)S(1)} %get-tuple-element.27), channel_id=1, replica_groups=mesh['ctx'=32,'tp'=8] {'ctx'}, dimensions={0} | all-to-all | bytes 655360 | tf_op jit(solution)/shard_map/all_to_all | solution.py:460
  35.4 6.7 %all-to-all-start.1 = ((bf16[32,32,128]{2,1,0:T(8,128)(2,1)}), bf16[32,32,128]{2,1,0:T(8,128)(2,1)S(1)}, u32[]{:S(2)}, u32[]{:S(2)}) async-start(bf16[32,32,128]{2,1,0:T(8,128)(2,1)} %mixer_scan.1), calls=%async_computation.1 | async-start | bytes 524288 | tf_op jit(solution)/shard_map/all_to_all | solution.py:466
  42.1 1.5 %collective-permute-start.5 = (bf16[512,128]{1,0:T(8,128)(2,1)S(1)}, bf16[512,128]{1,0:T(8,128)(2,1)S(1)}, u32[]{:S(2)}, u32[]{:S(2)}) collective-permute-start(bf16[512,128]{1,0:T(8,128)(2,1)S(1)} %get-tuple-element.34.refs_0_), channel_id=1, source_target_pairs={{0,8},{8,16},{16,24},{24,32},{32,40},{40,48},{48,56},{56,0},{64,72... | collective-permute-start | bytes 393224 | tf_op jit(solution)/shard_map/ppermute | solution.py:453
  43.6 1.8 %collective-permute-start.9 = (bf16[512,128]{1,0:T(8,128)(2,1)S(1)}, bf16[512,128]{1,0:T(8,128)(2,1)S(1)}, u32[]{:S(2)}, u32[]{:S(2)}) collective-permute-start(bf16[512,128]{1,0:T(8,128)(2,1)S(1)} %get-tuple-element.34.refs_0_), channel_id=1, source_target_pairs={{0,56},{8,0},{16,8},{24,16},{32,24},{40,32},{48,40},{56,48},{64,12... | collective-permute-start | bytes 393224 | tf_op jit(solution)/shard_map/ppermute | solution.py:454
  45.4 5.9 %collective-permute-done.5.refs_1_ = bf16[512,128]{1,0:T(8,128)(2,1)S(1)} collective-permute-done((bf16[512,128]{1,0:T(8,128)(2,1)S(1)}, bf16[512,128]{1,0:T(8,128)(2,1)S(1)}, u32[]{:S(2)}, u32[]{:S(2)}) %collective-permute-start.5) | collective-permute-done | bytes 131104 | tf_op jit(solution)/shard_map/ppermute | solution.py:453
  51.4 1.9 %mixer_inner.1.y0 = f32[256,1024]{1,0:T(8,128)S(1)} custom-call(f32[16]{0:T(128)S(1)} %copy-done.4, bf16[256,1024]{1,0:T(8,128)(2,1)S(1)} %get-tuple-element.23.xc, bf16[256,256]{1,0:T(8,128)(2,1)S(1)} %get-tuple-element.24.bc, f32[256,128]{1,0:T(8,128)S(1)} %get-tuple-element.25.cols, f32[32,256]{1,0:T(8,128)S(1)} %get-tuple-element.26.rows), custom_call_target="tpu_custom_call" | custom-call | tf_op jit(solution)/shard_map/mixer_inner/pallas_call | solution.py:152
  53.4 3.3 %collective-permute-start.10 = (bf16[512,128]{1,0:T(8,128)(2,1)S(1)}, bf16[512,128]{1,0:T(8,128)(2,1)S(1)}, u32[]{:S(2)}, u32[]{:S(2)}) collective-permute-start(bf16[512,128]{1,0:T(8,128)(2,1)S(1)} %collective-permute-done.9.refs_7_), channel_id=1, source_target_pairs={{0,56},{8,0},{16,8},{24,16},{32,24},{40,32},{48,40},{56,48},{64,12... | collective-permute-start | bytes 393224 | tf_op jit(solution)/shard_map/ppermute | solution.py:459
  57.9 5.8 %mixer_project.1 = (bf16[128,4096]{1,0:T(8,128)(2,1)S(1)}, bf16[128,4096]{1,0:T(8,128)(2,1)S(1)}) custom-call(s32[4]{0:T(128)S(1)} %pad_add_fusion.place, f32[256,1024]{1,0:T(8,128)S(1)} %mixer_inner.1.y0, bf16[256,256]{1,0:T(8,128)(2,1)S(1)} %get-tuple-element.24.bc, bf16[1024,128]{1,0:T(8,128)(2,1)S(1)} %bitcast.9, f32[256,128]{1,0:T(8,128)S(1)} %get-tuple-element.25.cols, ...), custom_call_target="tpu_custom_call" | custom-call | tf_op jit(solution)/shard_map/mixer_project/pallas_call | solution.py:202
  63.9 3.5 %collective-permute-start.11 = (bf16[512,128]{1,0:T(8,128)(2,1)S(1)}, bf16[512,128]{1,0:T(8,128)(2,1)S(1)}, u32[]{:S(2)}, u32[]{:S(2)}) collective-permute-start(bf16[512,128]{1,0:T(8,128)(2,1)S(1)} %collective-permute-done.10.refs_6_), channel_id=1, source_target_pairs={{0,56},{8,0},{16,8},{24,16},{32,24},{40,32},{48,40},{56,48},{64,12... | collective-permute-start | bytes 393224 | tf_op jit(solution)/shard_map/ppermute | solution.py:462
  67.4 3.1 %collective-permute-done.11.refs_5_ = bf16[512,128]{1,0:T(8,128)(2,1)S(1)} collective-permute-done((bf16[512,128]{1,0:T(8,128)(2,1)S(1)}, bf16[512,128]{1,0:T(8,128)(2,1)S(1)}, u32[]{:S(2)}, u32[]{:S(2)}) %collective-permute-start.11) | collective-permute-done | bytes 131104 | tf_op jit(solution)/shard_map/ppermute | solution.py:462
  70.5 3.4 %collective-permute-done.8.refs_4_ = bf16[512,128]{1,0:T(8,128)(2,1)S(1)} collective-permute-done((bf16[512,128]{1,0:T(8,128)(2,1)S(1)}, bf16[512,128]{1,0:T(8,128)(2,1)S(1)}, u32[]{:S(2)}, u32[]{:S(2)}) %collective-permute-start.8) | collective-permute-done | bytes 131104 | tf_op jit(solution)/shard_map/ppermute | solution.py:464
  74.6 1.3 stack_row.1
  76.0 1.4 %collective-permute-start.16 = (bf16[4,512,128]{2,1,0:T(8,128)(2,1)S(1)}, bf16[4,512,128]{2,1,0:T(8,128)(2,1)S(1)}, u32[]{:S(2)}, u32[]{:S(2)}) collective-permute-start(bf16[4,512,128]{2,1,0:T(8,128)(2,1)S(1)} %get-tuple-element.35), channel_id=1, source_target_pairs={{0,192},{8,200},{16,208},{24,216},{32,224},{40,232},{48,240},{56,2... | collective-permute-start | bytes 1572872 | tf_op jit(solution)/shard_map/ppermute | solution.py:472
  81.3 12.7 %collective-permute-done.16.refs_1_ = bf16[4,512,128]{2,1,0:T(8,128)(2,1)S(1)} collective-permute-done((bf16[4,512,128]{2,1,0:T(8,128)(2,1)S(1)}, bf16[4,512,128]{2,1,0:T(8,128)(2,1)S(1)}, u32[]{:S(2)}, u32[]{:S(2)}) %collective-permute-start.16) | collective-permute-done | bytes 524320 | tf_op jit(solution)/shard_map/ppermute | solution.py:472
  94.0 1.9 %collective-permute-start.17 = (bf16[4,512,128]{2,1,0:T(8,128)(2,1)S(1)}, bf16[4,512,128]{2,1,0:T(8,128)(2,1)S(1)}, u32[]{:S(2)}, u32[]{:S(2)}) collective-permute-start(bf16[4,512,128]{2,1,0:T(8,128)(2,1)S(1)} %collective-permute-done.16.refs_1_), channel_id=1, source_target_pairs={{192,128},{200,136},{208,144},{216,152},{224,160},{232,168},{240,1... | collective-permute-start | bytes 1572872 | tf_op jit(solution)/shard_map/ppermute | solution.py:475
  98.0 1.6 %collective-permute-start.2 = (bf16[32,4096]{1,0:T(8,128)(2,1)S(1)}, bf16[32,4096]{1,0:T(8,128)(2,1)S(1)}, u32[]{:S(2)}, u32[]{:S(2)}) collective-permute-start(bf16[32,4096]{1,0:T(8,128)(2,1)S(1)} %get-tuple-element.31), channel_id=1, source_target_pairs={{0,2},{1,3},{2,4},{3,5},{4,6},{5,7},{6,0},{7,1},{8,10},{9,11},{10,... | collective-permute-start | bytes 786440 | tf_op jit(solution)/shard_map/ppermute | solution.py:486
  99.6 5.7 %collective-permute-done.12.refs_0_ = bf16[4,512,128]{2,1,0:T(8,128)(2,1)S(1)} collective-permute-done((bf16[4,512,128]{2,1,0:T(8,128)(2,1)S(1)}, bf16[4,512,128]{2,1,0:T(8,128)(2,1)S(1)}, u32[]{:S(2)}, u32[]{:S(2)}) %collective-permute-start.12) | collective-permute-done | bytes 524320 | tf_op jit(solution)/shard_map/ppermute | solution.py:476
  105.3 3.0 %collective-permute-start.3 = (bf16[32,4096]{1,0:T(8,128)(2,1)S(1)}, bf16[32,4096]{1,0:T(8,128)(2,1)S(1)}, u32[]{:S(2)}, u32[]{:S(2)}) collective-permute-start(bf16[32,4096]{1,0:T(8,128)(2,1)S(1)} %get-tuple-element.32), channel_id=1, source_target_pairs={{0,4},{1,5},{2,6},{3,7},{4,0},{5,1},{6,2},{7,3},{8,12},{9,13},{10,... | collective-permute-start | bytes 786440 | tf_op jit(solution)/shard_map/ppermute | solution.py:486
  109.5 5.7 %attend_row.1 = (f32[8,8,256]{2,1,0:T(8,128)S(1)}, f32[8,136,256]{2,1,0:T(8,128)S(1)}) custom-call(s32[4]{0:T(128)S(1)} %pad_add_fusion.place, bf16[256,1024]{1,0:T(8,128)(2,1)S(1)} %copy-done, bf16[512,128]{1,0:T(8,128)(2,1)} %copy-done.2, bf16[512,128]{1,0:T(8,128)(2,1)} %copy-done.11, bf16[512,128]{1,0:T(8,128)(2,1)} %copy-done.13, ...), custom_call_target="tpu_custom_call" | custom-call | tf_op jit(solution)/shard_map/attend_row/pallas_call | solution.py:373
  115.3 6.5 %attend_rows.1 = (f32[8,8,256]{2,1,0:T(8,128)S(1)}, f32[8,136,256]{2,1,0:T(8,128)S(1)}) custom-call(s32[4]{0:T(128)S(1)} %pad_add_fusion.place, bf16[256,1024]{1,0:T(8,128)(2,1)S(1)} %copy-done, bf16[4,512,128]{2,1,0:T(8,128)(2,1)} %copy-done.8, bf16[4,512,128]{2,1,0:T(8,128)(2,1)} %copy-done.7, ...), custom_call_target="tpu_custom_call", output_to_operand_aliasing={{0}: (4, {}), {1}: (5, {})} | custom-call | tf_op jit(solution)/shard_map/attend_rows/pallas_call | solution.py:407
  122.7 12.4 %attend_final.1 = (bf16[256,1024]{1,0:T(8,128)(2,1)}, f32[8,8,256]{2,1,0:T(8,128)S(1)}, f32[8,136,256]{2,1,0:T(8,128)S(1)}) custom-call(s32[4]{0:T(128)S(1)} %pad_add_fusion.place, bf16[256,1024]{1,0:T(8,128)(2,1)S(1)} %copy-done, bf16[4,512,128]{2,1,0:T(8,128)(2,1)} %copy-done.5, ...), custom_call_target="tpu_custom_call", output_to_operand_aliasing={{1}: (6, {}), {2}: (7, {})} | custom-call | tf_op jit(solution)/shard_map/attend_final/pallas_call | solution.py:407
  (65 shorter events, 13.4 us)
Async XLA Ops:
  1.6 42.0 %copy-start.2 = (bf16[512,128]{1,0:T(8,128)(2,1)}, bf16[512,128]{1,0:T(8,128)(2,1)S(1)}, u32[]{:S(2)}) copy-start(bf16[512,128]{1,0:T(8,128)(2,1)S(1)} %get-tuple-element.34.refs_0_) | copy-start | bytes 393220
  1.7 9.7 %collective-permute-start = (bf16[8,1280]{1,0:T(8,128)(2,1)S(1)}, bf16[8,1280]{1,0:T(8,128)(2,1)S(1)}, u32[]{:S(2)}, u32[]{:S(2)}) collective-permute-start(bf16[8,1280]{1,0:T(8,128)(2,1)S(1)} %get-tuple-element.22), channel_id=1, source_target_pairs={{0,8},{8,16},{16,24},{24,32},{32,40},{40,48},{48,56},{56,64},{64,7... | collective-permute-start | bytes 61448 | tf_op jit(solution)/shard_map/ppermute | solution.py:452
  15.6 35.8 %copy-start.4 = (f32[16]{0:T(128)S(1)}, f32[16]{0:T(128)}, u32[]{:S(2)}) copy-start(f32[16]{0:T(128)} %skip.1) | copy-start | bytes 196
  35.4 22.5 %all-to-all-start.1 = ((bf16[32,32,128]{2,1,0:T(8,128)(2,1)}), bf16[32,32,128]{2,1,0:T(8,128)(2,1)S(1)}, u32[]{:S(2)}, u32[]{:S(2)}) async-start(bf16[32,32,128]{2,1,0:T(8,128)(2,1)} %mixer_scan.1), calls=%async_computation.1 | async-start | bytes 524288 | tf_op jit(solution)/shard_map/all_to_all | solution.py:466
  42.1 9.3 %collective-permute-start.5 = (bf16[512,128]{1,0:T(8,128)(2,1)S(1)}, bf16[512,128]{1,0:T(8,128)(2,1)S(1)}, u32[]{:S(2)}, u32[]{:S(2)}) collective-permute-start(bf16[512,128]{1,0:T(8,128)(2,1)S(1)} %get-tuple-element.34.refs_0_), channel_id=1, source_target_pairs={{0,8},{8,16},{16,24},{24,32},{32,40},{40,48},{48,56},{56,0},{64,72... | collective-permute-start | bytes 393224 | tf_op jit(solution)/shard_map/ppermute | solution.py:453
  43.6 9.7 %collective-permute-start.9 = (bf16[512,128]{1,0:T(8,128)(2,1)S(1)}, bf16[512,128]{1,0:T(8,128)(2,1)S(1)}, u32[]{:S(2)}, u32[]{:S(2)}) collective-permute-start(bf16[512,128]{1,0:T(8,128)(2,1)S(1)} %get-tuple-element.34.refs_0_), channel_id=1, source_target_pairs={{0,56},{8,0},{16,8},{24,16},{32,24},{40,32},{48,40},{56,48},{64,12... | collective-permute-start | bytes 393224 | tf_op jit(solution)/shard_map/ppermute | solution.py:454
  51.4 6.6 %collective-permute-start.6 = (bf16[512,128]{1,0:T(8,128)(2,1)S(1)}, bf16[512,128]{1,0:T(8,128)(2,1)S(1)}, u32[]{:S(2)}, u32[]{:S(2)}) collective-permute-start(bf16[512,128]{1,0:T(8,128)(2,1)S(1)} %collective-permute-done.5.refs_1_), channel_id=1, source_target_pairs={{0,8},{8,16},{16,24},{24,32},{32,40},{40,48},{48,56},{56,0},{64,72... | collective-permute-start | bytes 393224 | tf_op jit(solution)/shard_map/ppermute | solution.py:458
  53.4 10.5 %collective-permute-start.10 = (bf16[512,128]{1,0:T(8,128)(2,1)S(1)}, bf16[512,128]{1,0:T(8,128)(2,1)S(1)}, u32[]{:S(2)}, u32[]{:S(2)}) collective-permute-start(bf16[512,128]{1,0:T(8,128)(2,1)S(1)} %collective-permute-done.9.refs_7_), channel_id=1, source_target_pairs={{0,56},{8,0},{16,8},{24,16},{32,24},{40,32},{48,40},{56,48},{64,12... | collective-permute-start | bytes 393224 | tf_op jit(solution)/shard_map/ppermute | solution.py:459
  57.9 9.4 %collective-permute-start.7 = (bf16[512,128]{1,0:T(8,128)(2,1)S(1)}, bf16[512,128]{1,0:T(8,128)(2,1)S(1)}, u32[]{:S(2)}, u32[]{:S(2)}) collective-permute-start(bf16[512,128]{1,0:T(8,128)(2,1)S(1)} %collective-permute-done.6.refs_2_), channel_id=1, source_target_pairs={{0,8},{8,16},{16,24},{24,32},{32,40},{40,48},{48,56},{56,0},{64,72... | collective-permute-start | bytes 393224 | tf_op jit(solution)/shard_map/ppermute | solution.py:461
  63.8 33.5 %collective-permute-start.1 = (bf16[128,4096]{1,0:T(8,128)(2,1)S(1)}, bf16[128,4096]{1,0:T(8,128)(2,1)S(1)}, u32[]{:S(2)}, u32[]{:S(2)}) collective-permute-start(bf16[128,4096]{1,0:T(8,128)(2,1)S(1)} %get-tuple-element.29), channel_id=1, source_target_pairs={{0,1},{1,0},{2,3},{3,2},{4,5},{5,4},{6,7},{7,6},{8,9},{9,8},{10,11... | collective-permute-start | bytes 3145736 | tf_op jit(solution)/shard_map/ppermute | solution.py:482
  63.9 6.6 %collective-permute-start.11 = (bf16[512,128]{1,0:T(8,128)(2,1)S(1)}, bf16[512,128]{1,0:T(8,128)(2,1)S(1)}, u32[]{:S(2)}, u32[]{:S(2)}) collective-permute-start(bf16[512,128]{1,0:T(8,128)(2,1)S(1)} %collective-permute-done.10.refs_6_), channel_id=1, source_target_pairs={{0,56},{8,0},{16,8},{24,16},{32,24},{40,32},{48,40},{56,48},{64,12... | collective-permute-start | bytes 393224 | tf_op jit(solution)/shard_map/ppermute | solution.py:462
  67.4 6.6 %collective-permute-start.8 = (bf16[512,128]{1,0:T(8,128)(2,1)S(1)}, bf16[512,128]{1,0:T(8,128)(2,1)S(1)}, u32[]{:S(2)}, u32[]{:S(2)}) collective-permute-start(bf16[512,128]{1,0:T(8,128)(2,1)S(1)} %collective-permute-done.7.refs_3_), channel_id=1, source_target_pairs={{0,8},{8,16},{16,24},{24,32},{32,40},{40,48},{48,56},{56,0},{64,72... | collective-permute-start | bytes 393224 | tf_op jit(solution)/shard_map/ppermute | solution.py:464
  75.9 33.5 %copy-start = (bf16[256,1024]{1,0:T(8,128)(2,1)S(1)}, bf16[256,1024]{1,0:T(8,128)(2,1)}, u32[]{:S(2)}) copy-start(bf16[256,1024]{1,0:T(8,128)(2,1)} %q.5) | copy-start | bytes 1572868
  76.0 18.0 %collective-permute-start.16 = (bf16[4,512,128]{2,1,0:T(8,128)(2,1)S(1)}, bf16[4,512,128]{2,1,0:T(8,128)(2,1)S(1)}, u32[]{:S(2)}, u32[]{:S(2)}) collective-permute-start(bf16[4,512,128]{2,1,0:T(8,128)(2,1)S(1)} %get-tuple-element.35), channel_id=1, source_target_pairs={{0,192},{8,200},{16,208},{24,216},{32,224},{40,232},{48,240},{56,2... | collective-permute-start | bytes 1572872 | tf_op jit(solution)/shard_map/ppermute | solution.py:472
  77.4 18.5 %collective-permute-start.14 = (bf16[4,512,128]{2,1,0:T(8,128)(2,1)S(1)}, bf16[4,512,128]{2,1,0:T(8,128)(2,1)S(1)}, u32[]{:S(2)}, u32[]{:S(2)}) collective-permute-start(bf16[4,512,128]{2,1,0:T(8,128)(2,1)S(1)} %get-tuple-element.36), channel_id=1, source_target_pairs={{0,64},{8,72},{16,80},{24,88},{32,96},{40,104},{48,112},{56,120},{... | collective-permute-start | bytes 1572872 | tf_op jit(solution)/shard_map/ppermute | solution.py:471
  78.7 26.6 %collective-permute-start.12 = (bf16[4,512,128]{2,1,0:T(8,128)(2,1)S(1)}, bf16[4,512,128]{2,1,0:T(8,128)(2,1)S(1)}, u32[]{:S(2)}, u32[]{:S(2)}) collective-permute-start(bf16[4,512,128]{2,1,0:T(8,128)(2,1)S(1)} %get-tuple-element.35), channel_id=1, source_target_pairs={{0,64},{8,72},{16,80},{24,88},{32,96},{40,104},{48,112},{56,120},{... | collective-permute-start | bytes 1572872 | tf_op jit(solution)/shard_map/ppermute | solution.py:476
  80.0 28.4 %collective-permute-start.13 = (bf16[4,512,128]{2,1,0:T(8,128)(2,1)S(1)}, bf16[4,512,128]{2,1,0:T(8,128)(2,1)S(1)}, u32[]{:S(2)}, u32[]{:S(2)}) collective-permute-start(bf16[4,512,128]{2,1,0:T(8,128)(2,1)S(1)} %get-tuple-element.36), channel_id=1, source_target_pairs={{0,192},{8,200},{16,208},{24,216},{32,224},{40,232},{48,240},{56,2... | collective-permute-start | bytes 1572872 | tf_op jit(solution)/shard_map/ppermute | solution.py:477
  94.0 21.3 %copy-start.7 = (bf16[4,512,128]{2,1,0:T(8,128)(2,1)}, bf16[4,512,128]{2,1,0:T(8,128)(2,1)S(1)}, u32[]{:S(2)}) copy-start(bf16[4,512,128]{2,1,0:T(8,128)(2,1)S(1)} %collective-permute-done.16.refs_1_) | copy-start | bytes 1572868
  94.0 27.8 %collective-permute-start.17 = (bf16[4,512,128]{2,1,0:T(8,128)(2,1)S(1)}, bf16[4,512,128]{2,1,0:T(8,128)(2,1)S(1)}, u32[]{:S(2)}, u32[]{:S(2)}) collective-permute-start(bf16[4,512,128]{2,1,0:T(8,128)(2,1)S(1)} %collective-permute-done.16.refs_1_), channel_id=1, source_target_pairs={{192,128},{200,136},{208,144},{216,152},{224,160},{232,168},{240,1... | collective-permute-start | bytes 1572872 | tf_op jit(solution)/shard_map/ppermute | solution.py:475
  95.9 19.3 %copy-start.8 = (bf16[4,512,128]{2,1,0:T(8,128)(2,1)}, bf16[4,512,128]{2,1,0:T(8,128)(2,1)S(1)}, u32[]{:S(2)}) copy-start(bf16[4,512,128]{2,1,0:T(8,128)(2,1)S(1)} %collective-permute-done.14.refs_0_) | copy-start | bytes 1572868
  95.9 25.9 %collective-permute-start.15 = (bf16[4,512,128]{2,1,0:T(8,128)(2,1)S(1)}, bf16[4,512,128]{2,1,0:T(8,128)(2,1)S(1)}, u32[]{:S(2)}, u32[]{:S(2)}) collective-permute-start(bf16[4,512,128]{2,1,0:T(8,128)(2,1)S(1)} %collective-permute-done.14.refs_0_), channel_id=1, source_target_pairs={{64,128},{72,136},{80,144},{88,152},{96,160},{104,168},{112,176},{... | collective-permute-start | bytes 1572872 | tf_op jit(solution)/shard_map/ppermute | solution.py:474
  98.0 37.1 %collective-permute-start.2 = (bf16[32,4096]{1,0:T(8,128)(2,1)S(1)}, bf16[32,4096]{1,0:T(8,128)(2,1)S(1)}, u32[]{:S(2)}, u32[]{:S(2)}) collective-permute-start(bf16[32,4096]{1,0:T(8,128)(2,1)S(1)} %get-tuple-element.31), channel_id=1, source_target_pairs={{0,2},{1,3},{2,4},{3,5},{4,6},{5,7},{6,0},{7,1},{8,10},{9,11},{10,... | collective-permute-start | bytes 786440 | tf_op jit(solution)/shard_map/ppermute | solution.py:486
  105.3 29.9 %collective-permute-start.3 = (bf16[32,4096]{1,0:T(8,128)(2,1)S(1)}, bf16[32,4096]{1,0:T(8,128)(2,1)S(1)}, u32[]{:S(2)}, u32[]{:S(2)}) collective-permute-start(bf16[32,4096]{1,0:T(8,128)(2,1)S(1)} %get-tuple-element.32), channel_id=1, source_target_pairs={{0,4},{1,5},{2,6},{3,7},{4,0},{5,1},{6,2},{7,3},{8,12},{9,13},{10,... | collective-permute-start | bytes 786440 | tf_op jit(solution)/shard_map/ppermute | solution.py:486
  108.3 26.8 %collective-permute-start.4 = (bf16[32,4096]{1,0:T(8,128)(2,1)S(1)}, bf16[32,4096]{1,0:T(8,128)(2,1)S(1)}, u32[]{:S(2)}, u32[]{:S(2)}) collective-permute-start(bf16[32,4096]{1,0:T(8,128)(2,1)S(1)} %get-tuple-element.33), channel_id=1, source_target_pairs={{0,6},{1,7},{2,0},{3,1},{4,2},{5,3},{6,4},{7,5},{8,14},{9,15},{10,... | collective-permute-start | bytes 786440 | tf_op jit(solution)/shard_map/ppermute | solution.py:486
  (14 other events, 113.2 us)
